TPU v7x, 256 devices: a whole 4x4x8 slice. The times are simulated.
256 devices in a mesh: seq: 64 (over z, y, core), head: 4 (over x).
Axes of the slice: x: 4, y: 4, z: 8, core: 2. Of those that a mesh axis runs over, the one named last changes fastest.
Arguments:
- queries: bfloat16 [8192, 16, 128], P('seq', 'head'), may hold values from -6 to 6
- keys: bfloat16 [8192, 2, 16, 128], P('seq', None, 'head'), may hold values from -6 to 6
- values: bfloat16 [8192, 2, 16, 128], P('seq', None, 'head'), may hold values from -6 to 6
- betas: float32 [8192, 2, 16], P('seq', None, 'head'), may hold values from 0.5 to 2, as said below
- gain: float32 [128], replicated, may hold values from 0.1 to 1.9
- out_grad: bfloat16 [8192, 16, 128], P('seq', 'head'), may hold values from -6 to 6
Outputs:
- normed_out: bfloat16 [8192, 16, 128], P('seq', 'head')
- query_grad: bfloat16 [8192, 16, 128], P('seq', 'head')
- key_grad: bfloat16 [8192, 2, 16, 128], P('seq', None, 'head')
- value_grad: bfloat16 [8192, 2, 16, 128], P('seq', None, 'head')
- beta_grad: float32 [8192, 2, 16], P('seq', None, 'head')
- gain_grad: float32 [128], replicated
Inputs may be any that keep to these rules, and one draw needn't show every extreme that they name: `betas`: every step size lies strictly between 0 and 2.
All inputs are finite; a program needn't handle non-finite values.
Results may differ from a plain program's by a relative error of at most 0.003.
Values sent between devices are 32-bit elements; how exact they have to be, the bound alone decides.
A program may use at most 128 MiB of HBM per device.

v0:
```python
import jax
import jax.numpy as jnp
from jax import lax
from jax.sharding import PartitionSpec as P

GROUP = 128


EPS = 1e-06
HIGH_ACCURACY = lax.Precision.HIGHEST


def passed_along(value, axis, steps):
    count = lax.axis_size(axis)
    leading, last = (max(0, -steps), min(count, count - steps))
    return lax.ppermute(value, axis, [(source, source + steps) for source in range(leading, last)])


def prefix(array, axis, combine, identity):
    count, position = (lax.axis_size(axis), lax.axis_index(axis))
    everything = jax.tree.map(lambda part: lax.all_gather(part, axis), array)
    start = jax.tree.map(
        lambda part, zero: jnp.broadcast_to(jnp.asarray(zero, part.dtype), part.shape),
        array,
        identity,
    )

    def lap(k, before):
        at = count - 1 - k
        reached = at > position
        new = combine(before, jax.tree.map(lambda part: part[at], everything))
        return jax.tree.map(lambda a, b: jnp.where(reached, a, b), new, before)

    return lax.fori_loop(0, count, lap, start)


def unit_rows(vectors):
    return vectors * lax.rsqrt(jnp.sum(vectors * vectors, axis=-1, keepdims=True) + EPS)


def group_parts(group_offset, query_block_rows, key_block_rows, value_blk, beta_blk):
    group_width = key_block_rows.shape[1]
    half_width = query_block_rows.shape[1]
    key_dim = key_block_rows.shape[2]
    key_gram = jnp.einsum("hik,hjk->hij", key_block_rows, key_block_rows, precision=HIGH_ACCURACY)
    row_index = lax.broadcasted_iota(jnp.int32, (group_width, group_width), 0)
    col_index = lax.broadcasted_iota(jnp.int32, (group_width, group_width), 1)
    strict = (col_index < row_index).astype(jnp.float32)
    unit_lower = jnp.eye(group_width, dtype=jnp.float32) + beta_blk[:, :, None] * key_gram * strict
    right_side = jnp.concatenate(
        [beta_blk[:, :, None] * key_block_rows, beta_blk[:, :, None] * value_blk], axis=-1
    )
    solved = jax.scipy.linalg.solve_triangular(
        unit_lower, right_side, lower=True, unit_diagonal=True
    )
    weighted_keys = solved[:, :, :key_dim]
    corrected_values = solved[:, :, key_dim:]
    pseudo_values = corrected_values - jnp.einsum(
        "zsr,zrn->zsn", weighted_keys, group_offset, precision=HIGH_ACCURACY
    )
    token_index = lax.broadcasted_iota(jnp.int32, (half_width, group_width), 0)
    step_index = lax.broadcasted_iota(jnp.int32, (half_width, group_width), 1)
    visible = (step_index <= 2 * token_index + 1).astype(jnp.float32)
    scores = (
        jnp.einsum("htk,hck->htc", query_block_rows, key_block_rows, precision=HIGH_ACCURACY)
        * visible
    )
    output_rows = jnp.einsum(
        "asw,awl->asl", query_block_rows, group_offset, precision=HIGH_ACCURACY
    )
    output_rows = output_rows + jnp.einsum(
        "htc,hcv->htv", scores, pseudo_values, precision=HIGH_ACCURACY
    )
    final_state = group_offset + jnp.einsum(
        "yeb,yeo->ybo", key_block_rows, pseudo_values, precision=HIGH_ACCURACY
    )
    return (output_rows, final_state, weighted_keys, scores)


def group_apply(group_offset, query_block_rows, key_block_rows, value_blk, beta_blk):
    output_rows, final_state, weighted_keys, scores = group_parts(
        group_offset, query_block_rows, key_block_rows, value_blk, beta_blk
    )
    return (output_rows, final_state)


def compose(earlier, later):
    trans_early, state_early = earlier
    trans_late, state_late = later
    product = jnp.einsum("hij,hjk->hik", trans_late, trans_early, precision=HIGH_ACCURACY)
    carried = (
        jnp.einsum("hij,hjk->hik", trans_late, state_early, precision=HIGH_ACCURACY) + state_late
    )
    return (product, carried)


def local(queries, keys, values, betas, gain, out_grad):
    tok_local, heads_local, key_dim = queries.shape
    value_dim = values.shape[-1]
    substeps = keys.shape[1]
    group_width = GROUP
    half_width = group_width // substeps
    group_count = tok_local * substeps // group_width
    q_unit, q_pullback = jax.vjp(unit_rows, queries.astype(jnp.float32))
    k_unit, k_pullback = jax.vjp(unit_rows, keys.astype(jnp.float32))
    q_groups = q_unit.reshape(group_count, half_width, heads_local, key_dim).transpose(0, 2, 1, 3)
    k_groups = k_unit.reshape(group_count, group_width, heads_local, key_dim).transpose(0, 2, 1, 3)
    v_groups = (
        values.astype(jnp.float32)
        .reshape(group_count, group_width, heads_local, value_dim)
        .transpose(0, 2, 1, 3)
    )
    b_groups = betas.reshape(group_count, group_width, heads_local).transpose(0, 2, 1)
    grad_groups = (
        out_grad.astype(jnp.float32)
        .reshape(group_count, half_width, heads_local, value_dim)
        .transpose(0, 2, 1, 3)
    )
    eye_heads = jnp.broadcast_to(
        jnp.eye(key_dim, dtype=jnp.float32), (heads_local, key_dim, key_dim)
    )
    zero_state = jnp.zeros((heads_local, key_dim, value_dim), jnp.float32)

    def local_step(carry, items):
        local_state, transfer = carry
        query_block_rows, key_block_rows, value_blk, beta_blk = items
        output_rows, final_state, weighted_keys, scores = group_parts(
            local_state, query_block_rows, key_block_rows, value_blk, beta_blk
        )
        reduced = query_block_rows - jnp.einsum(
            "htc,hck->htk", scores, weighted_keys, precision=HIGH_ACCURACY
        )
        carried_rows = jnp.einsum("htk,hkj->htj", reduced, transfer, precision=HIGH_ACCURACY)
        weighted = jnp.einsum("hck,hkj->hcj", weighted_keys, transfer, precision=HIGH_ACCURACY)
        transfer_next = transfer - jnp.einsum(
            "hck,hcj->hkj", key_block_rows, weighted, precision=HIGH_ACCURACY
        )
        return ((final_state, transfer_next), (output_rows, carried_rows, local_state, transfer))

    group_inputs = (q_groups, k_groups, v_groups, b_groups)
    (shard_state, shard_trans), (local_out, carried_query_rows, local_starts, trans_starts) = (
        lax.scan(local_step, (zero_state, eye_heads), group_inputs)
    )
    seq_count = lax.axis_size("seq")

    def chain_turn(position, received):
        passed = (
            jnp.einsum("hij,hjk->hik", shard_trans, received, precision=HIGH_ACCURACY) + shard_state
        )
        return passed_along(passed, "seq", 1)

    entry_state = lax.fori_loop(0, seq_count - 1, chain_turn, zero_state)

    def replay_step(memory_matrix, items):
        block_out, final_state = group_apply(memory_matrix, *items)
        return (final_state, (block_out, memory_matrix))

    _, (output_rows, starts) = lax.scan(replay_step, entry_state, group_inputs)
    inv_rms = lax.rsqrt(jnp.mean(output_rows * output_rows, axis=-1, keepdims=True) + EPS)
    normal_out = output_rows * inv_rms
    normed = gain * normal_out
    gain_part = jnp.sum(grad_groups * normal_out, axis=(0, 1, 2))
    scaled_grad = grad_groups * gain
    output_adjoint = inv_rms * (
        scaled_grad - normal_out * jnp.mean(scaled_grad * normal_out, axis=-1, keepdims=True)
    )
    partition_adjoint = jnp.einsum(
        "beuc,beur->ecr", carried_query_rows, output_adjoint, precision=HIGH_ACCURACY
    )
    shard_trans_t = jnp.swapaxes(shard_trans, 1, 2)
    exit_adjoint = prefix(
        (shard_trans_t, partition_adjoint), "seq", compose, (eye_heads, zero_state)
    )[1]

    def back_step(adjoint, items):
        group_offset, query_block_rows, key_block_rows, value_blk, beta_blk, grad_blk = items
        _, pullback = jax.vjp(
            group_apply, group_offset, query_block_rows, key_block_rows, value_blk, beta_blk
        )
        d_start, d_query, d_key, d_value, d_beta = pullback((grad_blk, adjoint))
        return (d_start, (d_query, d_key, d_value, d_beta))

    _, (dq_groups, dk_groups, dv_groups, db_groups) = lax.scan(
        back_step,
        exit_adjoint,
        (starts, q_groups, k_groups, v_groups, b_groups, output_adjoint),
        reverse=True,
    )
    dq_unit = dq_groups.transpose(0, 2, 1, 3).reshape(tok_local, heads_local, key_dim)
    dk_unit = dk_groups.transpose(0, 2, 1, 3).reshape(tok_local, substeps, heads_local, key_dim)
    query_grad = q_pullback(dq_unit)[0].astype(jnp.bfloat16)
    key_grad = k_pullback(dk_unit)[0].astype(jnp.bfloat16)
    value_grad = (
        dv_groups.transpose(0, 2, 1, 3)
        .reshape(tok_local, substeps, heads_local, value_dim)
        .astype(jnp.bfloat16)
    )
    beta_grad = db_groups.transpose(0, 2, 1).reshape(tok_local, substeps, heads_local)
    normed_out = (
        normed.transpose(0, 2, 1, 3).reshape(tok_local, heads_local, value_dim).astype(jnp.bfloat16)
    )
    gain_grad = lax.psum(gain_part, ("seq", "head"))
    return (normed_out, query_grad, key_grad, value_grad, beta_grad, gain_grad)


def solution(mesh):
    return jax.shard_map(
        local,
        mesh=mesh,
        in_specs=(
            P("seq", "head", None),
            P("seq", None, "head", None),
            P("seq", None, "head", None),
            P("seq", None, "head"),
            P(),
            P("seq", "head", None),
        ),
        out_specs=(
            P("seq", "head", None),
            P("seq", "head", None),
            P("seq", None, "head", None),
            P("seq", None, "head", None),
            P("seq", None, "head"),
            P(),
        ),
        check_vma=False,
    )
```

profile of v0, /device:TPU:32, one launch (start us, length us, event | category | flops | bytes accessed | tf_op | source)
XLA Modules:
  0.0 1261.4 jit_solution(15787265287354406641)
XLA Ops:
  15.0 89.0 %while.80 = (s32[]{:T(128)}, f32[4,128,128]{2,1,0:T(8,128)S(1)}, f32[4,128,128]{2,1,0:T(8,128)S(1)}, f32[2,4,64,128]{3,2,1,0:T(8,128)S(1)}, f32[2,4,128,128]{3,2...) while((s32[]{:T(128)}, f32[4,128,128]{2,1,0:T(8,128)S(1)}, ...), condition=%wide.region_3.5_spmd.clone, body=%wide.region_2.4_spmd.clone.sunk | while | flops 856752384 | bytes 9022100 | solution.py:142
  16.0 39.3 %custom-call.28 = f32[4,1,128,128]{2,3,1,0:T(8,128)S(1)} custom-call(f32[4,1,128,128]{3,2,1,0:T(8,128)S(1)} %fusion.385), custom_call_target="InvertDiagBlocksLowerTriangular" | custom-call | tf_op jit(solution)/shard_map/while/body/eval_jaxpr/jit(_solve_triangular)/vmap()/triangular_solve/custom-call.1 | solution.py:53
  60.5 39.3 %custom-call.28 = f32[4,1,128,128]{2,3,1,0:T(8,128)S(1)} custom-call(f32[4,1,128,128]{3,2,1,0:T(8,128)S(1)} %fusion.385), custom_call_target="InvertDiagBlocksLowerTriangular" | custom-call | tf_op jit(solution)/shard_map/while/body/eval_jaxpr/jit(_solve_triangular)/vmap()/triangular_solve/custom-call.1 | solution.py:53
  105.8 658.8 %while.77 = (s32[]{:T(128)}, f32[4,128,128]{2,1,0:T(8,128)S(1)}, f32[4,128,128]{2,1,0:T(8,128)S(1)}, f32[4,128,128]{2,1,0:T(8,128)S(1)}, s32[]{:T(128)}) while((s32[]{:T(128)}, f32[4,128,128]{2,1,0:T(8,128)S(1)}, f32[4,128,128]{2,1,0:T(8,128)S(1)}, f32[4,128,128]{2,1,0:T(8,128)S(1)}, s32[]{:T(128)}) %tuple.178), condition=%wide.region_5.7_spmd, body=%wide.region_4.6_spmd.sunk | while | flops 100728832 | bytes 2097253 | solution.py:152
  108.1 7.9 collective-permute-done
  118.3 9.3 collective-permute-done
  130.0 9.6 collective-permute-done
  141.9 8.4 collective-permute-done
  152.7 7.9 collective-permute-done
  162.9 12.5 collective-permute-done
  177.7 11.2 collective-permute-done
  191.3 11.5 collective-permute-done
  205.1 8.6 collective-permute-done
  216.0 7.9 collective-permute-done
  226.2 7.9 collective-permute-done
  236.4 7.9 collective-permute-done
  246.6 7.9 collective-permute-done
  256.8 7.9 collective-permute-done
  267.0 7.9 collective-permute-done
  277.2 7.9 collective-permute-done
  287.4 7.9 collective-permute-done
  297.6 7.9 collective-permute-done
  307.8 7.9 collective-permute-done
  318.0 7.9 collective-permute-done
  328.2 7.9 collective-permute-done
  338.4 7.9 collective-permute-done
  348.6 7.9 collective-permute-done
  358.8 7.9 collective-permute-done
  369.0 7.9 collective-permute-done
  379.2 7.9 collective-permute-done
  389.4 7.9 collective-permute-done
  399.6 7.9 collective-permute-done
  409.8 7.9 collective-permute-done
  420.0 7.9 collective-permute-done
  430.2 7.9 collective-permute-done
  440.4 7.9 collective-permute-done
  450.6 7.9 collective-permute-done
  460.8 7.9 collective-permute-done
  471.0 7.9 collective-permute-done
  481.2 7.9 collective-permute-done
  491.4 7.9 collective-permute-done
  501.6 7.9 collective-permute-done
  511.8 7.9 collective-permute-done
  522.0 7.9 collective-permute-done
  532.2 7.9 collective-permute-done
  542.4 7.9 collective-permute-done
  552.6 7.9 collective-permute-done
  562.8 7.9 collective-permute-done
  573.0 7.9 collective-permute-done
  583.2 7.9 collective-permute-done
  593.4 7.9 collective-permute-done
  603.6 7.9 collective-permute-done
  613.8 7.9 collective-permute-done
  624.0 7.9 collective-permute-done
  634.2 7.9 collective-permute-done
  764.6 86.9 %while.78 = (s32[]{:T(128)}, f32[4,128,128]{2,1,0:T(8,128)S(1)}, f32[2,4,64,128]{3,2,1,0:T(8,128)S(1)}, f32[2,4,128,128]{3,2,1,0:T(8,128)S(1)}, f32[2,4,128,128]...) while((s32[]{:T(128)}, f32[4,128,128]{2,1,0:T(8,128)S(1)}, ...), condition=%wide.region_7.9_spmd, body=%wide.region_6.8_spmd.sunk | while | flops 655229184 | bytes 7711361 | solution.py:158
  766.0 39.3 %custom-call.26 = f32[4,1,128,128]{2,3,1,0:T(8,128)S(1)} custom-call(f32[4,1,128,128]{3,2,1,0:T(8,128)S(1)} %fusion.313), custom_call_target="InvertDiagBlocksLowerTriangular" | custom-call | tf_op jit(solution)/shard_map/while/body/eval_jaxpr/jit(_solve_triangular)/vmap()/triangular_solve/custom-call.1 | solution.py:53
  809.4 39.3 %custom-call.26 = f32[4,1,128,128]{2,3,1,0:T(8,128)S(1)} custom-call(f32[4,1,128,128]{3,2,1,0:T(8,128)S(1)} %fusion.313), custom_call_target="InvertDiagBlocksLowerTriangular" | custom-call | tf_op jit(solution)/shard_map/while/body/eval_jaxpr/jit(_solve_triangular)/vmap()/triangular_solve/custom-call.1 | solution.py:53
  857.1 154.4 %psum.7 = f32[128]{0:T(128)} all-reduce(f32[128]{0:T(128)S(1)} %get-tuple-element.715), channel_id=1, replica_groups=mesh['seq'=64,'head'=4] {'seq','head'}, use_global_device_ids=true, to_apply=%region_20.22 | all-reduce | flops 128 | bytes 1024 | tf_op jit(solution)/shard_map/psum | solution.py:202
  1012.3 23.2 %all-gather.7.cloned.1.call-done = f32[256,128,128]{2,1,0:T(8,128)} async-done(((f32[4,128,128]{2,1,0:T(8,128)}), f32[256,128,128]{2,1,0:T(8,128)}) %all-gather.7.cloned.1.call-update) | async-done | bytes 16777232 | tf_op jit(solution)/shard_map/all_gather | solution.py:21
  1035.4 95.1 %while.81 = (s32[]{:T(128)}, f32[4,128,128]{2,1,0:T(8,128)S(1)}, s32[]{:T(128)}, f32[64,4,128,128]{3,2,1,0:T(8,128)}, f32[64,4,128,128]{3,2,1,0:T(8,128)}, /*index=5*/s32[]{:T(128)}, s32[]{:T(128)}, s32[]{:T(128)}, s32[]{:T(128)}) while((s32[]{:T(128)}, f32[4,128,128]{2,1,0:T(8,128)S(1)}, s32[]{:T(128)}, ...), condition=%wide.region_11.13_spmd.clone, body=%wide.region_10.12_spmd.clone.sunk | while | flops 100925448 | bytes 1837733 | solution.py:34
  1132.2 110.0 %while.79 = (s32[]{:T(128)}, f32[4,128,128]{2,1,0:T(8,128)S(1)}, f32[2,4,64,128]{3,2,1,0:T(8,128)}, f32[2,4,128,128]{3,2,1,0:T(8,128)}, bf16[2,4,128,128]{3,2,1,...) while((s32[]{:T(128)}, f32[4,128,128]{2,1,0:T(8,128)S(1)}, ...), condition=%wide.region_16.18_spmd, body=%wide.region_12.17_spmd.sunk | while | flops 1864859392 | bytes 20173504 | solution.py:183
  1136.2 40.1 %custom-call.27 = f32[4,1,128,128]{2,3,1,0:T(8,128)S(1)} custom-call(f32[4,1,128,128]{3,2,1,0:T(8,128)} %add_bitcast_fusion.2), custom_call_target="InvertDiagBlocksLowerTriangular" | custom-call | tf_op jit(solution)/shard_map/while/body/eval_jaxpr/jvp(jit(_solve_triangular))/vmap()/triangular_solve/custom-call.1 | solution.py:53
  1191.2 40.1 %custom-call.27 = f32[4,1,128,128]{2,3,1,0:T(8,128)S(1)} custom-call(f32[4,1,128,128]{3,2,1,0:T(8,128)} %add_bitcast_fusion.2), custom_call_target="InvertDiagBlocksLowerTriangular" | custom-call | tf_op jit(solution)/shard_map/while/body/eval_jaxpr/jvp(jit(_solve_triangular))/vmap()/triangular_solve/custom-call.1 | solution.py:53
  (456 shorter events, 409.5 us)
Async XLA Ops:
  7.2 1005.1 %all-gather.5.cloned.1.call-start = ((), (), s32[]{:S(2)}) async-start(), calls=%async_computation | async-start | bytes 17039360 | tf_op jit(solution)/shard_map/all_gather | solution.py:21
  104.8 930.6 %all-gather.7.cloned.1.call-start = ((), (), s32[]{:S(2)}) async-start(), calls=%async_computation.1 | async-start | bytes 17039360 | tf_op jit(solution)/shard_map/all_gather | solution.py:21
  106.2 9.8 collective-permute-start
  116.4 11.3 collective-permute-start
  128.0 11.6 collective-permute-start
  140.0 10.3 collective-permute-start
  150.7 9.8 collective-permute-start
  160.9 14.5 %collective-permute-start = (f32[4,128,128]{2,1,0:T(8,128)S(1)}, f32[4,128,128]{2,1,0:T(8,128)S(1)}, u32[]{:S(2)}, u32[]{:S(2)}) collective-permute-start(f32[4,128,128]{2,1,0:T(8,128)S(1)} %convolution_add_fusion.19), channel_id=1, source_target_pairs={{0,4},{4,8},{8,12},{12,16},{16,20},{20,24},{24,28},{28,32},{32,36}... | collective-permute-start | bytes 786440 | tf_op jit(solution)/shard_map/while/body/eval_jaxpr/ppermute | solution.py:16
  175.8 13.1 %collective-permute-start = (f32[4,128,128]{2,1,0:T(8,128)S(1)}, f32[4,128,128]{2,1,0:T(8,128)S(1)}, u32[]{:S(2)}, u32[]{:S(2)}) collective-permute-start(f32[4,128,128]{2,1,0:T(8,128)S(1)} %convolution_add_fusion.19), channel_id=1, source_target_pairs={{0,4},{4,8},{8,12},{12,16},{16,20},{20,24},{24,28},{28,32},{32,36}... | collective-permute-start | bytes 786440 | tf_op jit(solution)/shard_map/while/body/eval_jaxpr/ppermute | solution.py:16
  189.3 13.4 %collective-permute-start = (f32[4,128,128]{2,1,0:T(8,128)S(1)}, f32[4,128,128]{2,1,0:T(8,128)S(1)}, u32[]{:S(2)}, u32[]{:S(2)}) collective-permute-start(f32[4,128,128]{2,1,0:T(8,128)S(1)} %convolution_add_fusion.19), channel_id=1, source_target_pairs={{0,4},{4,8},{8,12},{12,16},{16,20},{20,24},{24,28},{28,32},{32,36}... | collective-permute-start | bytes 786440 | tf_op jit(solution)/shard_map/while/body/eval_jaxpr/ppermute | solution.py:16
  203.2 10.5 collective-permute-start
  214.1 9.8 collective-permute-start
  224.3 9.8 collective-permute-start
  234.5 9.8 collective-permute-start
  244.7 9.8 collective-permute-start
  254.9 9.8 collective-permute-start
  265.1 9.8 collective-permute-start
  275.3 9.8 collective-permute-start
  285.5 9.8 collective-permute-start
  295.7 9.8 collective-permute-start
  305.9 9.8 collective-permute-start
  316.1 9.8 collective-permute-start
  326.3 9.8 collective-permute-start
  336.5 9.8 collective-permute-start
  346.7 9.8 collective-permute-start
  356.9 9.8 collective-permute-start
  367.1 9.8 collective-permute-start
  377.3 9.8 collective-permute-start
  387.5 9.8 collective-permute-start
  397.7 9.8 collective-permute-start
  407.9 9.8 collective-permute-start
  418.1 9.8 collective-permute-start
  428.3 9.8 collective-permute-start
  438.5 9.8 collective-permute-start
  448.7 9.8 collective-permute-start
  458.9 9.8 collective-permute-start
  469.1 9.8 collective-permute-start
  479.3 9.8 collective-permute-start
  489.5 9.8 collective-permute-start
  499.7 9.8 collective-permute-start
  509.9 9.8 collective-permute-start
  520.1 9.8 collective-permute-start
  530.3 9.8 collective-permute-start
  540.5 9.8 collective-permute-start
  550.7 9.8 collective-permute-start
  560.9 9.8 collective-permute-start
  571.1 9.8 collective-permute-start
  581.3 9.8 collective-permute-start
  591.5 9.8 collective-permute-start
  601.7 9.8 collective-permute-start
  611.9 9.8 collective-permute-start
  622.1 9.8 collective-permute-start
  632.3 9.8 collective-permute-start
  642.5 9.8 collective-permute-start
  652.7 9.8 collective-permute-start
  662.9 9.8 collective-permute-start
  673.1 9.8 collective-permute-start
  683.3 9.8 collective-permute-start
  693.5 9.8 collective-permute-start
  703.7 9.8 collective-permute-start
  713.9 9.8 collective-permute-start
  724.1 9.8 collective-permute-start
  734.3 9.8 collective-permute-start
  744.5 9.8 collective-permute-start
  (6 other events, 854.8 us)
Sparse Core Ops, SparseCore 0:
  104.9 108.4 all-gather.4
  856.4 178.9 all-gather.6
where the time goes:
time: 1270 us; the launch traced here: 1260 us
  waiting for transfers between devices  535 us (42%)
  other arithmetic  258 us (20%)
  matrix products  160 us (13%)
  blocking collectives  154 us (12%)
  starting transfers between devices  121 us (10%)
  between operations  14.4 us (1%)
  local copies, waits for them, and re-layouts  13.5 us (1%)
    ppermute x63, waiting for transfers between devices, passed_along(): lax.ppermute(value, axis, [(source, source + steps) for source in range(l...  512 us
    another operation x20, other arithmetic, group_parts(): jax.scipy.linalg.solve_triangular(unit_lower, right_side, lower=True, uni...  240 us
    psum x1, blocking collectives, local(): gain_grad = lax.psum(gain_part, ('seq', 'head'))  154 us
    ppermute x63, starting transfers between devices, passed_along(): lax.ppermute(value, axis, [(source, source + steps) for source in range(l...  121 us
    dot_general x64, matrix products, compose(): jnp.einsum('hij,hjk->hik', trans_late, state_early, precision=HIGH_ACCURACY)  91.1 us
  transfers between devices with their start and end apart: 65, of which 64 were waited for; matrix products, arithmetic and copies ran while one was open for 9% of the time, Pallas kernels for 0%

commit v1 on v0

v1 whole, which is shorter than its diff:
```python
import functools

import jax
import jax.numpy as jnp
from jax import lax
from jax.experimental import pallas as pl
from jax.experimental.pallas import tpu as pltpu
from jax.sharding import PartitionSpec as P

EPS = 1e-06
F32 = jnp.float32
BF16 = jnp.bfloat16
MESH = pl.DeviceIdType.MESH
NY = 4
NZ = 8
NC = 2


def split(x):
    hi = x.astype(BF16)
    lo = (x - hi.astype(F32)).astype(BF16)
    return hi, lo


def dot(a, b, dims):
    return lax.dot_general(a, b, (dims, ((), ())), preferred_element_type=F32)


def mm(a, b, ca=1, cb=0):
    ah, al = split(a)
    bh, bl = split(b)
    left = jnp.concatenate([ah, al, ah], axis=ca)
    right = jnp.concatenate([bh, bh, bl], axis=cb)
    return dot(left, right, ((ca,), (cb,)))


def iotas(rows, cols):
    return (
        lax.broadcasted_iota(jnp.int32, (rows, cols), 0),
        lax.broadcasted_iota(jnp.int32, (rows, cols), 1),
    )


def unit_pullback(d_unit, unit, inverse):
    return (d_unit - unit * jnp.sum(unit * d_unit, axis=-1, keepdims=True)) * inverse


def kernel(
    q_ref, k_ref, v_ref, b_ref, g_ref, do_ref,
    out_ref, dq_ref, dk_ref, dv_ref, db_ref, dg_ref,
    ku_s, qu_s, rk_s, rq_s, n_s, w_s, u_s, sc_s, r_s, ol_s, p_s, adj_s,
    ab_s, pair_s, comp_s, own_s, phi_s, beta_s, zab_s, za_s, sout_s, sin_s, s1_s,
    aown_s, phi0_s, theta_s, psi_s, c_s, cpair_s, cc_s, cown_s, crow_s, zc_s, gam_s, dsend_s, dout_s, d0_s,
    gpart_s, grow_s, gz_s, gx_s, gsum_s,
    send_sem, pair_sem, own_sem, zab_sem, za_sem, sin_sem, aown_sem, cpair_sem, cown_sem, zc_sem, dout_sem,
    gsend_sem, grow_sem, gz_sem, gx_sem,
):
    heads = q_ref.shape[1]
    tok = q_ref.shape[0]
    steps = k_ref.shape[0]
    dim = q_ref.shape[2]
    seq = lax.axis_index("seq")
    xpos = lax.axis_index("head")
    z = seq // (NY * NC)
    y = (seq // NC) % NY
    c = seq % NC

    def dev(zz, yy, cc):
        return {"seq": zz * (NY * NC) + yy * NC + cc}

    barrier = pltpu.get_barrier_semaphore()
    count = 0
    for dy in range(NY):
        for dc in range(NC):
            if dy or dc:
                pl.semaphore_signal(
                    barrier, inc=1, device_id=dev(z, (y + dy) % NY, (c + dc) % NC), device_id_type=MESH
                )
                count += 1
    for dz in range(1, NZ):
        for dc in range(NC):
            pl.semaphore_signal(
                barrier, inc=1, device_id=dev((z + dz) % NZ, y, (c + dc) % NC), device_id_type=MESH
            )
            count += 1
    for dx in range(1, 4):
        pl.semaphore_signal(
            barrier, inc=1, device_id={"head": (xpos + dx) % 4}, device_id_type=MESH
        )
        count += 1

    def remote(src, dst, ssem, rsem, target):
        return pltpu.make_async_remote_copy(
            src_ref=src, dst_ref=dst, send_sem=ssem, recv_sem=rsem, device_id=target, device_id_type=MESH
        )

    def arrived(dst, rsem):
        pltpu.make_async_copy(dst, dst, rsem).wait()

    row_i, col_i = iotas(steps, steps)
    tok_i, step_i = iotas(tok, steps)
    visible = step_i <= 2 * tok_i + 1
    eye = (row_i == col_i).astype(F32)
    eye_dim = eye[:dim, :dim]

    for dlt in range(1, NZ):
        @pl.when(z < dlt)
        def _():
            zab_s[dlt - 1] = jnp.zeros((2, dim, dim), F32)

        @pl.when(z + dlt >= NZ)
        def _():
            za_s[dlt - 1] = jnp.zeros((dim, dim), F32)
            zc_s[dlt - 1] = jnp.zeros((dim, dim), F32)

    for h in range(heads):
        q = q_ref[:, h, :].astype(F32)
        k = k_ref[:, h, :].astype(F32)
        v = v_ref[:, h, :].astype(F32)
        b = b_ref[:, h:h + 1]
        rq = lax.rsqrt(jnp.sum(q * q, axis=-1, keepdims=True) + EPS)
        rk = lax.rsqrt(jnp.sum(k * k, axis=-1, keepdims=True) + EPS)
        qu = q * rq
        ku = k * rk
        gram = mm(ku, ku, 1, 1)
        low = jnp.where(col_i < row_i, gram * b, 0.0)
        inv = eye - jnp.where(row_i // 2 == col_i // 2, low, 0.0)
        size = 2
        while size < steps:
            band = (row_i // (2 * size) == col_i // (2 * size)) & (row_i // size != col_i // size)
            inv = inv - mm(inv, mm(jnp.where(band, low, 0.0), inv))
            size *= 2
        wu = mm(inv, jnp.concatenate([b * ku, b * v], axis=1))
        ab = mm(ku, wu, 0, 0)
        ab_s[h, 0] = eye_dim - ab[:, :dim]
        ab_s[h, 1] = ab[:, dim:]
        sc = jnp.where(visible, mm(qu, ku, 1, 1), 0.0)
        ro = mm(sc, wu)
        ku_s[h] = ku
        qu_s[h] = qu
        rk_s[h] = rk
        rq_s[h] = rq
        n_s[h] = inv
        w_s[h] = wu[:, :dim]
        u_s[h] = wu[:, dim:]
        sc_s[h] = sc
        r_s[h] = qu - ro[:, :dim]
        ol_s[h] = ro[:, dim:]

    pl.semaphore_wait(barrier, count)

    other = 1 - c
    pair = dev(z, y, other)
    send = {}
    for j in range(2):
        send["pair", j] = remote(
            ab_s.at[2 * other + j], pair_s.at[j], send_sem.at[j], pair_sem.at[j], pair
        )
        send["pair", j].start()
    for j in range(2):
        arrived(pair_s.at[j], pair_sem.at[j])
        mine = ab_s[2 * c + j]
        theirs = pair_s[j]
        first = jnp.where(c == 0, mine, theirs)
        second = jnp.where(c == 0, theirs, mine)
        both = mm(second[0], jnp.concatenate([first[0], first[1]], axis=1))
        comp_s[j, 0] = both[:, :dim]
        comp_s[j, 1] = both[:, dim:] + second[1]
        head = 2 * c + j
        here = (c == 1) & (y == head)

        @pl.when(here)
        def _():
            pltpu.make_async_copy(comp_s.at[j], own_s.at[y], own_sem.at[y]).start()

        @pl.when(jnp.logical_not(here))
        def _():
            remote(comp_s.at[j], own_s.at[y], send_sem.at[2 + j], own_sem.at[y], dev(z, head, 1)).start()

    @pl.when(c == 1)
    def _():
        low_core = dev(z, y, 0)
        arrived(own_s.at[0], own_sem.at[0])
        x = jnp.concatenate([own_s[0, 0], own_s[0, 1]], axis=1)
        phi_s[0] = x[:, :dim]
        beta_s[0] = x[:, dim:]
        for i in range(1, NY):
            arrived(own_s.at[i], own_sem.at[i])
            x = mm(own_s[i, 0], x)
            x = jnp.concatenate([x[:, :dim], x[:, dim:] + own_s[i, 1]], axis=1)
            phi_s[i] = x[:, :dim]
            beta_s[i] = x[:, dim:]
        comp_row = own_s.at[0]
        comp_row[0] = x[:, :dim]
        comp_row[1] = x[:, dim:]
        for dlt in range(NZ - 1, 0, -1):
            @pl.when(z + dlt < NZ)
            def _():
                remote(
                    own_s.at[0], zab_s.at[dlt - 1], send_sem.at[4 + dlt], zab_sem.at[dlt - 1],
                    dev(z + dlt, y, 1),
                ).start()
        for dlt in range(1, NZ):
            @pl.when(z >= dlt)
            def _():
                remote(
                    phi_s.at[NY - 1], za_s.at[dlt - 1], send_sem.at[12 + dlt], za_sem.at[dlt - 1],
                    dev(z - dlt, y, 0),
                ).start()
        for i in range(1, NY):
            remote(own_s.at[i, 0], aown_s.at[i], send_sem.at[20 + i], aown_sem.at[i], low_core).start()
            remote(phi_s.at[i - 1], phi0_s.at[i], send_sem.at[24 + i], aown_sem.at[NY + i], low_core).start()
        state = jnp.zeros((dim, dim), F32)
        for dlt in range(NZ - 1, 0, -1):
            @pl.when(z >= dlt)
            def _():
                arrived(zab_s.at[dlt - 1], zab_sem.at[dlt - 1])

            if dlt == NZ - 1:
                state = zab_s[dlt - 1, 1]
            else:
                state = mm(zab_s[dlt - 1, 0], state) + zab_s[dlt - 1, 1]
        sout_s[0] = state
        later = mm(jnp.concatenate([phi_s[i] for i in range(NY - 1)], axis=0), state)
        for i in range(1, NY):
            sout_s[i] = later[(i - 1) * dim:i * dim] + beta_s[i - 1]
        for i in range(NY):
            remote(sout_s.at[i], sin_s.at[y], send_sem.at[28 + i], sin_sem.at[y], dev(z, i, 0)).start()
        for h in range(heads):
            arrived(sin_s.at[h], sin_sem.at[h])

    @pl.when(c == 0)
    def _():
        for i in range(1, NY):
            arrived(aown_s.at[i], aown_sem.at[i])
            arrived(phi0_s.at[i], aown_sem.at[NY + i])
        psi_s[NY - 2] = aown_s[NY - 1]
        for i in range(NY - 3, -1, -1):
            psi_s[i] = mm(psi_s[i + 1], aown_s[i + 1])
        theta_s[0] = eye_dim
        for dlt in range(1, NZ - 1):
            @pl.when(z + dlt < NZ)
            def _():
                arrived(za_s.at[dlt - 1], za_sem.at[dlt - 1])

            theta_s[dlt] = za_s[0] if dlt == 1 else mm(za_s[dlt - 1], theta_s[dlt - 1])

        @pl.when(z + NZ - 1 < NZ)
        def _():
            arrived(za_s.at[NZ - 2], za_sem.at[NZ - 2])

        for h in range(heads):
            arrived(sin_s.at[h], sin_sem.at[h])
            s1_s[h] = mm(ab_s[h, 0], sin_s[h]) + ab_s[h, 1]
            remote(s1_s.at[h], sin_s.at[h], send_sem.at[28 + h], sin_sem.at[h], pair).start()

    gain = g_ref[...]
    gain_part = jnp.zeros((1, dim), F32)
    for h in range(heads):
        state = sin_s[h]
        both = mm(jnp.concatenate([r_s[h], w_s[h]], axis=0), state)
        o = ol_s[h] + both[:tok]
        p_s[h] = u_s[h] - both[tok:]
        inv_rms = lax.rsqrt(jnp.mean(o * o, axis=-1, keepdims=True) + EPS)
        normal = o * inv_rms
        grad = do_ref[:, h, :].astype(F32)
        out_ref[:, h, :] = (gain * normal).astype(BF16)
        gain_part = gain_part + jnp.sum(grad * normal, axis=0, keepdims=True)
        scaled = grad * gain
        adj = inv_rms * (scaled - normal * jnp.mean(scaled * normal, axis=-1, keepdims=True))
        adj_s[h] = adj
        c_s[h] = mm(r_s[h], adj, 0, 0)

        @pl.when(c == 1)
        def _():
            remote(c_s.at[h], cpair_s.at[h], send_sem.at[32 + h], cpair_sem.at[h], pair).start()

    gpart_s[...] = jnp.broadcast_to(gain_part, (8, dim))
    me8 = y * NC + c
    n_g = 0
    gsends = []
    for d in range(1, NY * NC):
        to = (me8 + d) % (NY * NC)
        gsends.append(remote(
            gpart_s, grow_s.at[me8], gsend_sem.at[n_g], grow_sem.at[d - 1], dev(z, to // NC, to % NC)))
        gsends[-1].start()
        n_g += 1
    grow_s[me8] = gpart_s[...]

    @pl.when(c == 0)
    def _():
        for h in range(heads):
            arrived(cpair_s.at[h], cpair_sem.at[h])
            cc_s[h] = mm(ab_s[h, 0], cpair_s[h], 0, 0) + c_s[h]

            @pl.when(y == h)
            def _():
                pltpu.make_async_copy(cc_s.at[h], cown_s.at[h], cown_sem.at[h]).start()

            @pl.when(y != h)
            def _():
                remote(cc_s.at[h], cown_s.at[y], send_sem.at[32 + h], cown_sem.at[y], dev(z, h, 0)).start()
        for i in range(NY):
            arrived(cown_s.at[i], cown_sem.at[i])
        left = jnp.concatenate([phi0_s[i] for i in range(1, NY)], axis=0)
        right = jnp.concatenate([cown_s[i] for i in range(1, NY)], axis=0)
        crow_s[...] = cown_s[0] + mm(left, right, 0, 0)
        for dlt in range(NZ - 1, 0, -1):
            @pl.when(z >= dlt)
            def _():
                remote(
                    crow_s, zc_s.at[dlt - 1], send_sem.at[4 + dlt], zc_sem.at[dlt - 1], dev(z - dlt, y, 0)
                ).start()
        gam_s[NY - 2] = cown_s[NY - 1]
        for i in range(NY - 3, -1, -1):
            gam_s[i] = mm(aown_s[i + 1], gam_s[i + 1], 0, 0) + cown_s[i + 1]
        for dlt in range(NZ - 1, 0, -1):
            @pl.when(z + dlt < NZ)
            def _():
                arrived(zc_s.at[dlt - 1], zc_sem.at[dlt - 1])
        left = jnp.concatenate([theta_s[i] for i in range(1, NZ - 1)], axis=0)
        right = jnp.concatenate([zc_s[i] for i in range(1, NZ - 1)], axis=0)
        d_row = zc_s[0] + mm(left, right, 0, 0)
        dsend_s[NY - 1] = d_row
        for i in range(NY - 1):
            dsend_s[i] = mm(psi_s[i], d_row, 0, 0) + gam_s[i]
        for i in range(NY):
            remote(dsend_s.at[i], dout_s.at[y], send_sem.at[12 + i], dout_sem.at[y], dev(z, i, 1)).start()
        for h in range(heads):
            arrived(dout_s.at[h], dout_sem.at[h])

    @pl.when(c == 1)
    def _():
        for h in range(heads):
            arrived(dout_s.at[h], dout_sem.at[h])
            d0_s[h] = mm(ab_s[h, 0], dout_s[h], 0, 0) + c_s[h]
            remote(d0_s.at[h], dout_s.at[h], send_sem.at[36 + h], dout_sem.at[h], pair).start()

    for d in range(1, NY * NC):
        fr = (me8 + NY * NC - d) % (NY * NC)
        arrived(grow_s.at[fr], grow_sem.at[d - 1])
    gsum_s[0] = jnp.sum(grow_s[...], axis=0)
    for d in range(1, NZ):
        gsends.append(remote(
            gsum_s.at[0], gz_s.at[z], gsend_sem.at[n_g], gz_sem.at[d - 1], dev((z + d) % NZ, y, c)))
        gsends[-1].start()
        n_g += 1
    gz_s[z] = gsum_s[0]

    lane = lax.broadcasted_iota(jnp.int32, (steps, heads), 1)
    db_all = jnp.zeros((steps, heads), F32)
    for h in range(heads):
        ku = ku_s[h]
        qu = qu_s[h]
        p = p_s[h]
        adj = adj_s[h]
        b = b_ref[:, h:h + 1]
        state = sin_s[h]
        d_out = dout_s[h]
        m_do = jnp.where(visible, mm(adj, p, 1, 1), 0.0)
        dq = mm(adj, state, 1, 1) + mm(m_do, ku)
        dp = mm(sc_s[h], adj, 0, 0) + mm(ku, d_out)
        gm = mm(n_s[h], dp, 0, 0)
        dv = b * gm
        db = jnp.sum(gm * p, axis=-1, keepdims=True) / b
        hm = jnp.where(col_i < row_i, mm(dv, p, 1, 1), 0.0)
        dk = mm(m_do, qu, 0, 0) + mm(p, d_out, 1, 1) - mm(dv, state, 1, 1) - mm(hm, ku) - mm(hm, ku, 0, 0)
        dq_ref[:, h, :] = unit_pullback(dq, qu, rq_s[h]).astype(BF16)
        dk_ref[:, h, :] = unit_pullback(dk, ku, rk_s[h]).astype(BF16)
        dv_ref[:, h, :] = dv.astype(BF16)
        db_all = db_all + jnp.where(lane == h, db, 0.0)
    db_ref[...] = db_all

    for d in range(1, NZ):
        arrived(gz_s.at[(z + NZ - d) % NZ], gz_sem.at[d - 1])
    gsum_s[1] = jnp.sum(gz_s[...], axis=0)
    for d in range(1, 4):
        gsends.append(remote(
            gsum_s.at[1], gx_s.at[xpos], gsend_sem.at[n_g], gx_sem.at[d - 1], {"head": (xpos + d) % 4}))
        gsends[-1].start()
        n_g += 1
    gx_s[xpos] = gsum_s[1]
    for d in range(1, 4):
        arrived(gx_s.at[(xpos + 4 - d) % 4], gx_sem.at[d - 1])
    dg_ref[...] = jnp.sum(gx_s[...], axis=0)[0:1]

    for j in range(2):
        send["pair", j].wait_send()
        head = 2 * c + j

        @pl.when(jnp.logical_not((c == 1) & (y == head)))
        def _():
            remote(comp_s.at[j], own_s.at[y], send_sem.at[2 + j], own_sem.at[y], dev(z, head, 1)).wait_send()

    def left(src, sem):
        remote(src, src, sem, sem, pair).wait_send()

    @pl.when(c == 1)
    def _():
        for dlt in range(1, NZ):
            @pl.when(z + dlt < NZ)
            def _():
                left(own_s.at[0], send_sem.at[4 + dlt])

            @pl.when(z >= dlt)
            def _():
                left(phi_s.at[NY - 1], send_sem.at[12 + dlt])
        for i in range(1, NY):
            left(own_s.at[i, 0], send_sem.at[20 + i])
            left(phi_s.at[i - 1], send_sem.at[24 + i])
        for i in range(NY):
            left(sout_s.at[i], send_sem.at[28 + i])
            left(c_s.at[i], send_sem.at[32 + i])
            left(d0_s.at[i], send_sem.at[36 + i])

    @pl.when(c == 0)
    def _():
        for h in range(heads):
            left(s1_s.at[h], send_sem.at[28 + h])

            @pl.when(y != h)
            def _():
                left(cc_s.at[h], send_sem.at[32 + h])
        for dlt in range(1, NZ):
            @pl.when(z >= dlt)
            def _():
                left(crow_s, send_sem.at[4 + dlt])
        for i in range(NY):
            left(dsend_s.at[i], send_sem.at[12 + i])
    for copy in gsends:
        copy.wait_send()


def local(queries, keys, values, betas, gain, out_grad):
    tok, heads, dim = queries.shape
    steps = tok * keys.shape[1]
    f = lambda *s: pltpu.VMEM(s, F32)
    dma = pltpu.SemaphoreType.DMA
    vmem = pl.BlockSpec(memory_space=pltpu.VMEM)
    scratch = [
        f(heads, steps, dim), f(heads, tok, dim), f(heads, steps, 1), f(heads, tok, 1),
        f(heads, steps, steps), f(heads, steps, dim), f(heads, steps, dim), f(heads, tok, steps),
        f(heads, tok, dim), f(heads, tok, dim), f(heads, steps, dim), f(heads, tok, dim),
        f(heads, 2, dim, dim), f(2, 2, dim, dim), f(2, 2, dim, dim), f(NY, 2, dim, dim),
        f(NY, dim, dim), f(NY, dim, dim), f(NZ - 1, 2, dim, dim), f(NZ - 1, dim, dim),
        f(NY, dim, dim), f(heads, dim, dim), f(heads, dim, dim),
        f(NY, dim, dim), f(NY, dim, dim), f(NZ - 1, dim, dim), f(NY - 1, dim, dim), f(heads, dim, dim),
        f(heads, dim, dim), f(heads, dim, dim), f(NY, dim, dim), f(dim, dim), f(NZ - 1, dim, dim),
        f(NY - 1, dim, dim), f(NY, dim, dim), f(heads, dim, dim), f(heads, dim, dim),
        f(8, dim), f(NY * NC, 8, dim), f(NZ, 8, dim), f(4, 8, dim), f(2, 8, dim),
        dma((40,)), dma((2,)), dma((NY,)), dma((NZ - 1,)), dma((NZ - 1,)), dma((heads,)), dma((2 * NY,)),
        dma((heads,)), dma((NY,)), dma((NZ - 1,)), dma((heads,)),
        dma((24,)), dma((NY * NC - 1,)), dma((NZ - 1,)), dma((3,)),
    ]
    outs = pl.pallas_call(
        kernel,
        out_shape=(
            jax.ShapeDtypeStruct((tok, heads, dim), BF16),
            jax.ShapeDtypeStruct((tok, heads, dim), BF16),
            jax.ShapeDtypeStruct((steps, heads, dim), BF16),
            jax.ShapeDtypeStruct((steps, heads, dim), BF16),
            jax.ShapeDtypeStruct((steps, heads), F32),
            jax.ShapeDtypeStruct((1, dim), F32),
        ),
        in_specs=[vmem] * 6,
        out_specs=(vmem,) * 6,
        scratch_shapes=scratch,
        compiler_params=pltpu.CompilerParams(
            collective_id=0, has_side_effects=True, vmem_limit_bytes=60 * 1024 * 1024
        ),
        name="delta_product",
    )(
        queries,
        keys.reshape(steps, heads, dim),
        values.reshape(steps, heads, dim),
        betas.reshape(steps, heads),
        gain.reshape(1, dim),
        out_grad,
    )
    out, dq, dk, dv, db, dg = outs
    return (out, dq, dk.reshape(keys.shape), dv.reshape(values.shape), db.reshape(betas.shape), dg.reshape(dim))


def solution(mesh):
    return jax.shard_map(
        local,
        mesh=mesh,
        in_specs=(
            P("seq", "head", None),
            P("seq", None, "head", None),
            P("seq", None, "head", None),
            P("seq", None, "head"),
            P(),
            P("seq", "head", None),
        ),
        out_specs=(
            P("seq", "head", None),
            P("seq", "head", None),
            P("seq", None, "head", None),
            P("seq", None, "head", None),
            P("seq", None, "head"),
            P(),
        ),
        check_vma=False,
    )
```

time: 1270 us -> 93.5 us (0.07)
  waiting for transfers between devices: 535 us -> 0 us
  other arithmetic: 258 us -> 0 us
  matrix products: 160 us -> 0 us
  blocking collectives: 154 us -> 0 us
  starting transfers between devices: 121 us -> 0 us
  Pallas kernels: 0 us -> 85.4 us
  between operations: 14.4 us -> 0.67 us
    ppermute x63 -> x0, waiting for transfers between devices: 512 us -> none  [passed_along(): lax.ppermute(value, axis, [(source, source + steps) for source in range(l...]
    another operation x20 -> x0, other arithmetic: 240 us -> none  [group_parts(): jax.scipy.linalg.solve_triangular(unit_lower, right_side, lower=True, uni...]
    psum x1 -> x0, blocking collectives: 154 us -> none  [local(): gain_grad = lax.psum(gain_part, ('seq', 'head'))]
    dot_general x188 -> x0, matrix products: 153 us -> none  [the longest x64 91.1 us: compose(): jnp.einsum('hij,hjk->hik', trans_late, state_early, precision=HIGH_ACCURACY)]
    ppermute x63 -> x0, starting transfers between devices: 121 us -> none  [passed_along(): lax.ppermute(value, axis, [(source, source + steps) for source in range(l...]
    pallas_call x0 -> x1, Pallas kernels: none -> 85.4 us  [local(): pl.pallas_call(kernel, out_shape=(jax.ShapeDtypeStruct((tok, heads, dim),...]
    all_gather x2 -> x0, waiting for transfers between devices: 23.2 us -> none  [prefix(): everything = jax.tree.map(lambda part: lax.all_gather(part, axis), array)]
  transfers between devices with their start and end apart: 65 -> 0, of which waited for: 64 -> 0; matrix products, arithmetic and copies ran while one was open for 9% -> 0% of each run, Pallas kernels for 0% -> 0%
where the time goes in v1:
time: 93.5 us; the launch traced here: 92.8 us
  Pallas kernels  85.4 us (91%)
  local copies, waits for them, and re-layouts  6.68 us (7%)
    pallas_call x1, Pallas kernels, local(): pl.pallas_call(kernel, out_shape=(jax.ShapeDtypeStruct((tok, heads, dim),...  85.4 us
    unnamed x19, local copies, waits for them, and re-layouts  6.68 us

profile of v1, /device:TPU:32, one launch (start us, length us, event | category | flops | bytes accessed | tf_op | source)
XLA Modules:
  0.0 92.8 jit_solution(11691811290323299090)
XLA Ops:
  0.6 0.0 copy-start.4
  0.6 0.7 copy-done.4
  1.3 0.8 copy.12
  2.1 85.4 %delta_product.1 = (bf16[128,4,128]{2,1,0:T(4,128)(2,1)}, bf16[128,4,128]{2,1,0:T(4,128)(2,1)}, bf16[256,4,128]{2,1,0:T(4,128)(2,1)}, bf16[256,4,128]{2,1,0:T(4,...) custom-call(bf16[128,4,128]{2,1,0:T(4,128)(2,1)} %q_ref.1, bf16[256,4,128]{2,1,0:T(4,128)(2,1)} %bitcast.9, ...), custom_call_target="tpu_custom_call" | custom-call | tf_op jit(solution)/shard_map/delta_product/pallas_call | solution.py:455
  87.6 0.0 copy-start.3
  87.6 0.0 copy-start.2
  87.6 1.6 %copy.13 = f32[128,2,4]{0,2,1:T(4,128)} copy(f32[128,2,4]{2,1,0:T(2,128)} %bitcast.13) | data formatting | bytes 8192
  89.2 0.0 copy-done.3
  89.2 0.0 copy-start.1
  89.2 0.7 copy.19
  89.9 0.0 copy-done.2
  89.9 0.7 copy.20
  90.5 0.0 copy-done.1
  90.5 0.0 copy-start
  90.5 0.7 copy.21
  91.2 0.3 copy-done
  91.6 0.0 copy-start.5
  91.6 0.7 copy.22
  92.3 0.0 copy-done.5
  92.3 0.5 copy.23
Async XLA Ops:
  0.6 0.7 copy-start.4
  87.6 1.6 %copy-start.3 = (bf16[128,4,128]{2,1,0:T(4,128)(2,1)S(1)}, bf16[128,4,128]{2,1,0:T(4,128)(2,1)}, u32[]{:S(2)}) copy-start(bf16[128,4,128]{2,1,0:T(4,128)(2,1)} %get-tuple-element.30) | copy-start | bytes 393220
  87.6 2.3 %copy-start.2 = (bf16[128,4,128]{2,1,0:T(4,128)(2,1)S(1)}, bf16[128,4,128]{2,1,0:T(4,128)(2,1)}, u32[]{:S(2)}) copy-start(bf16[128,4,128]{2,1,0:T(4,128)(2,1)} %get-tuple-element.31) | copy-start | bytes 393220
  89.2 1.3 %copy-start.1 = (bf16[256,4,128]{2,1,0:T(4,128)(2,1)S(1)}, bf16[256,4,128]{2,1,0:T(4,128)(2,1)}, u32[]{:S(2)}) copy-start(bf16[256,4,128]{2,1,0:T(4,128)(2,1)} %get-tuple-element.14) | copy-start | bytes 786436
  90.5 1.0 %copy-start = (bf16[256,4,128]{2,1,0:T(4,128)(2,1)S(1)}, bf16[256,4,128]{2,1,0:T(4,128)(2,1)}, u32[]{:S(2)}) copy-start(bf16[256,4,128]{2,1,0:T(4,128)(2,1)} %get-tuple-element.15) | copy-start | bytes 786436
  91.6 0.7 copy-start.5

commit v2 on v1

--- a/solution.py
+++ b/solution.py
@@ -26,12 +26,14 @@
     return lax.dot_general(a, b, (dims, ((), ())), preferred_element_type=F32)
 
 
+def mms(a, b, ca=1, cb=0):
+    left = jnp.concatenate([a[0], a[1], a[0]], axis=ca)
+    right = jnp.concatenate([b[0], b[0], b[1]], axis=cb)
+    return dot(left, right, ((ca,), (cb,)))
+
+
 def mm(a, b, ca=1, cb=0):
-    ah, al = split(a)
-    bh, bl = split(b)
-    left = jnp.concatenate([ah, al, ah], axis=ca)
-    right = jnp.concatenate([bh, bh, bl], axis=cb)
-    return dot(left, right, ((ca,), (cb,)))
+    return mms(split(a), split(b), ca, cb)
 
 
 def iotas(rows, cols):
@@ -48,17 +50,17 @@
 def kernel(
     q_ref, k_ref, v_ref, b_ref, g_ref, do_ref,
     out_ref, dq_ref, dk_ref, dv_ref, db_ref, dg_ref,
-    ku_s, qu_s, rk_s, rq_s, n_s, w_s, u_s, sc_s, r_s, ol_s, p_s, adj_s,
+    ku_s, qu_s, vf_s, dof_s, rk_s, rq_s, low_s, n_s, nt_s, nk_s, wu_s, sct_s, r_s, rt_s, ol_s, p_s, adj_s,
+    g0_s, dk1_s, of_s, dq_s, dk_s, dvf_s,
     ab_s, pair_s, comp_s, own_s, phi_s, beta_s, zab_s, za_s, sout_s, sin_s, s1_s,
     aown_s, phi0_s, theta_s, psi_s, c_s, cpair_s, cc_s, cown_s, crow_s, zc_s, gam_s, dsend_s, dout_s, d0_s,
     gpart_s, grow_s, gz_s, gx_s, gsum_s,
     send_sem, pair_sem, own_sem, zab_sem, za_sem, sin_sem, aown_sem, cpair_sem, cown_sem, zc_sem, dout_sem,
     gsend_sem, grow_sem, gz_sem, gx_sem,
 ):
-    heads = q_ref.shape[1]
-    tok = q_ref.shape[0]
-    steps = k_ref.shape[0]
-    dim = q_ref.shape[2]
+    steps, heads = b_ref.shape
+    tok = q_ref.shape[0] // heads
+    dim = q_ref.shape[1]
     seq = lax.axis_index("seq")
     xpos = lax.axis_index("head")
     z = seq // (NY * NC)
@@ -113,39 +115,104 @@
             za_s[dlt - 1] = jnp.zeros((dim, dim), F32)
             zc_s[dlt - 1] = jnp.zeros((dim, dim), F32)
 
+    q = q_ref[...].astype(F32)
+    k = k_ref[...].astype(F32)
+    rq = lax.rsqrt(jnp.sum(q * q, axis=-1, keepdims=True) + EPS)
+    rk = lax.rsqrt(jnp.sum(k * k, axis=-1, keepdims=True) + EPS)
+    rq_s[...] = rq
+    rk_s[...] = rk
+    qu_s[...] = q * rq
+    ku_s[...] = k * rk
+    vf_s[...] = v_ref[...].astype(F32)
+    dof_s[...] = do_ref[...].astype(F32)
+
+    def of_head(ref, h, rows):
+        return ref[pl.ds(h, rows, stride=heads), :]
+
+    half = steps // 2
+    base = 16
+    blocks = half // base
+    lane16 = lax.broadcasted_iota(jnp.int32, (base, half), 1) // base
+    packed = []
     for h in range(heads):
-        q = q_ref[:, h, :].astype(F32)
-        k = k_ref[:, h, :].astype(F32)
-        v = v_ref[:, h, :].astype(F32)
+        ku = of_head(ku_s, h, steps)
         b = b_ref[:, h:h + 1]
-        rq = lax.rsqrt(jnp.sum(q * q, axis=-1, keepdims=True) + EPS)
-        rk = lax.rsqrt(jnp.sum(k * k, axis=-1, keepdims=True) + EPS)
-        qu = q * rq
-        ku = k * rk
-        gram = mm(ku, ku, 1, 1)
-        low = jnp.where(col_i < row_i, gram * b, 0.0)
-        inv = eye - jnp.where(row_i // 2 == col_i // 2, low, 0.0)
-        size = 2
-        while size < steps:
-            band = (row_i // (2 * size) == col_i // (2 * size)) & (row_i // size != col_i // size)
-            inv = inv - mm(inv, mm(jnp.where(band, low, 0.0), inv))
-            size *= 2
-        wu = mm(inv, jnp.concatenate([b * ku, b * v], axis=1))
-        ab = mm(ku, wu, 0, 0)
+        low = jnp.where(col_i < row_i, mm(ku, ku, 1, 1) * b, 0.0)
+        low_s[h] = low
+        for part in range(2):
+            tri = low[part * half:(part + 1) * half, part * half:(part + 1) * half]
+            diag = jnp.zeros((base, half), F32)
+            for i in range(blocks):
+                diag = jnp.where(lane16 == i, tri[i * base:(i + 1) * base], diag)
+            packed.append(diag)
+    packed = jnp.concatenate(packed, axis=0)
+    rows = packed.shape[0]
+    lane = lax.broadcasted_iota(jnp.int32, (rows, half), 1)
+    row = lax.broadcasted_iota(jnp.int32, (rows, half), 0)
+    inv = jnp.where(row % base == lane % base, 1.0, 0.0)
+    for step in range(base - 1):
+        column = jnp.take_along_axis(packed, (lane // base) * base + step, axis=1)
+        pivot = inv.reshape(rows // base, base, half)[:, step:step + 1, :]
+        pivot = jnp.broadcast_to(pivot, (rows // base, base, half)).reshape(rows, half)
+        inv = inv - column * pivot
+    quads = [(h, part) for h in range(heads) for part in range(2)]
+    for n, (h, part) in enumerate(quads):
+        mine = inv[n * base:(n + 1) * base]
+        n_s[h, part * half:(part + 1) * half, part * half:(part + 1) * half] = jnp.concatenate(
+            [jnp.where(lane16 == i, mine, 0.0) for i in range(blocks)], axis=0
+        )
+        if part:
+            n_s[h, 0:half, half:steps] = jnp.zeros((half, half), F32)
+    sub_i, sub_j = row_i[:half, :half], col_i[:half, :half]
+    size = base
+    while size < half:
+        band = (sub_i // (2 * size) == sub_j // (2 * size)) & (sub_i // size != sub_j // size)
+        firsts = {}
+        for h, part in quads:
+            at = pl.ds(part * half, half)
+            parts = split(n_s[h, at, at])
+            firsts[h, part] = parts, mms(split(low_s[h, at, at]), parts)
+        for h, part in quads:
+            at = pl.ds(part * half, half)
+            parts, first = firsts[h, part]
+            n_s[h, at, at] = n_s[h, at, at] - jnp.where(band, mms(parts, split(first)), 0.0)
+        size *= 2
+    firsts = [mm(low_s[h, half:steps, 0:half], n_s[h, 0:half, 0:half]) for h in range(heads)]
+    for h in range(heads):
+        n_s[h, half:steps, 0:half] = -mm(n_s[h, half:steps, half:steps], firsts[h])
+    for h in range(heads):
+        ku = of_head(ku_s, h, steps)
+        b = b_ref[:, h:h + 1]
+        wu_s[h] = mm(n_s[h], jnp.concatenate([b * ku, b * of_head(vf_s, h, steps)], axis=1))
+    for h in range(heads):
+        ab = mm(of_head(ku_s, h, steps).T, wu_s[h])
         ab_s[h, 0] = eye_dim - ab[:, :dim]
         ab_s[h, 1] = ab[:, dim:]
-        sc = jnp.where(visible, mm(qu, ku, 1, 1), 0.0)
-        ro = mm(sc, wu)
-        ku_s[h] = ku
-        qu_s[h] = qu
-        rk_s[h] = rk
-        rq_s[h] = rq
-        n_s[h] = inv
-        w_s[h] = wu[:, :dim]
-        u_s[h] = wu[:, dim:]
-        sc_s[h] = sc
-        r_s[h] = qu - ro[:, :dim]
-        ol_s[h] = ro[:, dim:]
+
+    def fill_forward():
+        for h in range(heads):
+            ku = of_head(ku_s, h, steps)
+            qu = of_head(qu_s, h, tok)
+            sc = jnp.where(visible, mm(qu, ku, 1, 1), 0.0)
+            ro = mm(sc, wu_s[h])
+            r = qu - ro[:, :dim]
+            r_s[h] = r
+            rt_s[h] = r.T
+            ol_s[h] = ro[:, dim:]
+            sct_s[h] = sc.T
+            nt = n_s[h].T
+            nt_s[h] = nt
+            nk_s[h] = mm(nt, ku)
+
+    def fill_backward():
+        for h in range(heads):
+            ku = of_head(ku_s, h, steps)
+            adj = adj_s[h]
+            m_do = jnp.where(visible, mm(adj, p_s[h], 1, 1), 0.0)
+            dq = mm(adj, sin_s[h], 1, 1) + mm(m_do, ku)
+            dq_s[pl.ds(h, tok, stride=heads), :] = dq
+            dk1_s[h] = mm(m_do.T, of_head(qu_s, h, tok))
+            g0_s[h] = mm(nt_s[h], mm(sct_s[h], adj))
 
     pl.semaphore_wait(barrier, count)
 
@@ -210,6 +277,7 @@
         for i in range(1, NY):
             remote(own_s.at[i, 0], aown_s.at[i], send_sem.at[20 + i], aown_sem.at[i], low_core).start()
             remote(phi_s.at[i - 1], phi0_s.at[i], send_sem.at[24 + i], aown_sem.at[NY + i], low_core).start()
+        fill_forward()
         state = jnp.zeros((dim, dim), F32)
         for dlt in range(NZ - 1, 0, -1):
             @pl.when(z >= dlt)
@@ -231,6 +299,7 @@
 
     @pl.when(c == 0)
     def _():
+        fill_forward()
         for i in range(1, NY):
             arrived(aown_s.at[i], aown_sem.at[i])
             arrived(phi0_s.at[i], aown_sem.at[NY + i])
@@ -258,18 +327,18 @@
     gain_part = jnp.zeros((1, dim), F32)
     for h in range(heads):
         state = sin_s[h]
-        both = mm(jnp.concatenate([r_s[h], w_s[h]], axis=0), state)
+        both = mm(jnp.concatenate([r_s[h], wu_s[h, :, :dim]], axis=0), state)
         o = ol_s[h] + both[:tok]
-        p_s[h] = u_s[h] - both[tok:]
+        p_s[h] = wu_s[h, :, dim:] - both[tok:]
         inv_rms = lax.rsqrt(jnp.mean(o * o, axis=-1, keepdims=True) + EPS)
         normal = o * inv_rms
-        grad = do_ref[:, h, :].astype(F32)
-        out_ref[:, h, :] = (gain * normal).astype(BF16)
+        grad = of_head(dof_s, h, tok)
+        of_s[pl.ds(h, tok, stride=heads), :] = gain * normal
         gain_part = gain_part + jnp.sum(grad * normal, axis=0, keepdims=True)
         scaled = grad * gain
         adj = inv_rms * (scaled - normal * jnp.mean(scaled * normal, axis=-1, keepdims=True))
         adj_s[h] = adj
-        c_s[h] = mm(r_s[h], adj, 0, 0)
+        c_s[h] = mm(rt_s[h], adj)
 
         @pl.when(c == 1)
         def _():
@@ -287,6 +356,25 @@
         n_g += 1
     grow_s[me8] = gpart_s[...]
 
+    def gain_along_z():
+        for d in range(1, NY * NC):
+            fr = (me8 + NY * NC - d) % (NY * NC)
+            arrived(grow_s.at[fr], grow_sem.at[d - 1])
+        gsum_s[0] = jnp.sum(grow_s[...], axis=0)
+        for d in range(1, NZ):
+            gz_copy(d).start()
+        gz_s[z] = gsum_s[0]
+
+    def gz_copy(d):
+        return remote(
+            gsum_s.at[0], gz_s.at[z], gsend_sem.at[6 + d], gz_sem.at[d - 1], dev((z + d) % NZ, y, c)
+        )
+
+    def gx_copy(d):
+        return remote(
+            gsum_s.at[1], gx_s.at[xpos], gsend_sem.at[13 + d], gx_sem.at[d - 1], {"head": (xpos + d) % 4}
+        )
+
     @pl.when(c == 0)
     def _():
         for h in range(heads):
@@ -314,6 +402,8 @@
         gam_s[NY - 2] = cown_s[NY - 1]
         for i in range(NY - 3, -1, -1):
             gam_s[i] = mm(aown_s[i + 1], gam_s[i + 1], 0, 0) + cown_s[i + 1]
+        gain_along_z()
+        fill_backward()
         for dlt in range(NZ - 1, 0, -1):
             @pl.when(z + dlt < NZ)
             def _():
@@ -331,55 +421,42 @@
 
     @pl.when(c == 1)
     def _():
+        gain_along_z()
+        fill_backward()
         for h in range(heads):
             arrived(dout_s.at[h], dout_sem.at[h])
             d0_s[h] = mm(ab_s[h, 0], dout_s[h], 0, 0) + c_s[h]
             remote(d0_s.at[h], dout_s.at[h], send_sem.at[36 + h], dout_sem.at[h], pair).start()
-
-    for d in range(1, NY * NC):
-        fr = (me8 + NY * NC - d) % (NY * NC)
-        arrived(grow_s.at[fr], grow_sem.at[d - 1])
-    gsum_s[0] = jnp.sum(grow_s[...], axis=0)
-    for d in range(1, NZ):
-        gsends.append(remote(
-            gsum_s.at[0], gz_s.at[z], gsend_sem.at[n_g], gz_sem.at[d - 1], dev((z + d) % NZ, y, c)))
-        gsends[-1].start()
-        n_g += 1
-    gz_s[z] = gsum_s[0]
-
-    lane = lax.broadcasted_iota(jnp.int32, (steps, heads), 1)
-    db_all = jnp.zeros((steps, heads), F32)
-    for h in range(heads):
-        ku = ku_s[h]
-        qu = qu_s[h]
-        p = p_s[h]
-        adj = adj_s[h]
-        b = b_ref[:, h:h + 1]
-        state = sin_s[h]
-        d_out = dout_s[h]
-        m_do = jnp.where(visible, mm(adj, p, 1, 1), 0.0)
-        dq = mm(adj, state, 1, 1) + mm(m_do, ku)
-        dp = mm(sc_s[h], adj, 0, 0) + mm(ku, d_out)
-        gm = mm(n_s[h], dp, 0, 0)
-        dv = b * gm
-        db = jnp.sum(gm * p, axis=-1, keepdims=True) / b
-        hm = jnp.where(col_i < row_i, mm(dv, p, 1, 1), 0.0)
-        dk = mm(m_do, qu, 0, 0) + mm(p, d_out, 1, 1) - mm(dv, state, 1, 1) - mm(hm, ku) - mm(hm, ku, 0, 0)
-        dq_ref[:, h, :] = unit_pullback(dq, qu, rq_s[h]).astype(BF16)
-        dk_ref[:, h, :] = unit_pullback(dk, ku, rk_s[h]).astype(BF16)
-        dv_ref[:, h, :] = dv.astype(BF16)
-        db_all = db_all + jnp.where(lane == h, db, 0.0)
-    db_ref[...] = db_all
 
     for d in range(1, NZ):
         arrived(gz_s.at[(z + NZ - d) % NZ], gz_sem.at[d - 1])
     gsum_s[1] = jnp.sum(gz_s[...], axis=0)
     for d in range(1, 4):
-        gsends.append(remote(
-            gsum_s.at[1], gx_s.at[xpos], gsend_sem.at[n_g], gx_sem.at[d - 1], {"head": (xpos + d) % 4}))
-        gsends[-1].start()
-        n_g += 1
+        gx_copy(d).start()
     gx_s[xpos] = gsum_s[1]
+
+    lane = lax.broadcasted_iota(jnp.int32, (steps, heads), 1)
+    db_all = jnp.zeros((steps, heads), F32)
+    for h in range(heads):
+        p = p_s[h]
+        b = b_ref[:, h:h + 1]
+        d_out = dout_s[h]
+        gm = g0_s[h] + mm(nk_s[h], d_out)
+        dv = b * gm
+        dvf_s[pl.ds(h, steps, stride=heads), :] = dv
+        db = jnp.sum(gm * p, axis=-1, keepdims=True) / b
+        db_all = db_all + jnp.where(lane == h, db, 0.0)
+        hm = jnp.where(col_i < row_i, mm(dv, p, 1, 1), 0.0)
+        dk = dk1_s[h] + mm(
+            jnp.concatenate([p, dv], axis=1), jnp.concatenate([d_out, -sin_s[h]], axis=1), 1, 1
+        ) - mm(hm + hm.T, of_head(ku_s, h, steps))
+        dk_s[pl.ds(h, steps, stride=heads), :] = dk
+    db_ref[...] = db_all
+    out_ref[...] = of_s[...].astype(BF16)
+    dq_ref[...] = unit_pullback(dq_s[...], qu_s[...], rq_s[...]).astype(BF16)
+    dk_ref[...] = unit_pullback(dk_s[...], ku_s[...], rk_s[...]).astype(BF16)
+    dv_ref[...] = dvf_s[...].astype(BF16)
+
     for d in range(1, 4):
         arrived(gx_s.at[(xpos + 4 - d) % 4], gx_sem.at[d - 1])
     dg_ref[...] = jnp.sum(gx_s[...], axis=0)[0:1]
@@ -429,6 +506,10 @@
             left(dsend_s.at[i], send_sem.at[12 + i])
     for copy in gsends:
         copy.wait_send()
+    for d in range(1, NZ):
+        gz_copy(d).wait_send()
+    for d in range(1, 4):
+        gx_copy(d).wait_send()
 
 
 def local(queries, keys, values, betas, gain, out_grad):
@@ -438,9 +519,12 @@
     dma = pltpu.SemaphoreType.DMA
     vmem = pl.BlockSpec(memory_space=pltpu.VMEM)
     scratch = [
-        f(heads, steps, dim), f(heads, tok, dim), f(heads, steps, 1), f(heads, tok, 1),
-        f(heads, steps, steps), f(heads, steps, dim), f(heads, steps, dim), f(heads, tok, steps),
-        f(heads, tok, dim), f(heads, tok, dim), f(heads, steps, dim), f(heads, tok, dim),
+        f(steps * heads, dim), f(tok * heads, dim), f(steps * heads, dim), f(tok * heads, dim),
+        f(steps * heads, 1), f(tok * heads, 1), f(heads, steps, steps), f(heads, steps, steps),
+        f(heads, steps, steps), f(heads, steps, dim), f(heads, steps, 2 * dim), f(heads, steps, tok),
+        f(heads, tok, dim), f(heads, dim, tok), f(heads, tok, dim), f(heads, steps, dim), f(heads, tok, dim),
+        f(heads, steps, dim), f(heads, steps, dim), f(tok * heads, dim), f(tok * heads, dim),
+        f(steps * heads, dim), f(steps * heads, dim),
         f(heads, 2, dim, dim), f(2, 2, dim, dim), f(2, 2, dim, dim), f(NY, 2, dim, dim),
         f(NY, dim, dim), f(NY, dim, dim), f(NZ - 1, 2, dim, dim), f(NZ - 1, dim, dim),
         f(NY, dim, dim), f(heads, dim, dim), f(heads, dim, dim),
@@ -455,10 +539,10 @@
     outs = pl.pallas_call(
         kernel,
         out_shape=(
-            jax.ShapeDtypeStruct((tok, heads, dim), BF16),
-            jax.ShapeDtypeStruct((tok, heads, dim), BF16),
-            jax.ShapeDtypeStruct((steps, heads, dim), BF16),
-            jax.ShapeDtypeStruct((steps, heads, dim), BF16),
+            jax.ShapeDtypeStruct((tok * heads, dim), BF16),
+            jax.ShapeDtypeStruct((tok * heads, dim), BF16),
+            jax.ShapeDtypeStruct((steps * heads, dim), BF16),
+            jax.ShapeDtypeStruct((steps * heads, dim), BF16),
             jax.ShapeDtypeStruct((steps, heads), F32),
             jax.ShapeDtypeStruct((1, dim), F32),
         ),
@@ -470,15 +554,17 @@
         ),
         name="delta_product",
     )(
-        queries,
-        keys.reshape(steps, heads, dim),
-        values.reshape(steps, heads, dim),
+        queries.reshape(tok * heads, dim),
+        keys.reshape(steps * heads, dim),
+        values.reshape(steps * heads, dim),
         betas.reshape(steps, heads),
         gain.reshape(1, dim),
-        out_grad,
+        out_grad.reshape(tok * heads, dim),
     )
     out, dq, dk, dv, db, dg = outs
-    return (out, dq, dk.reshape(keys.shape), dv.reshape(values.shape), db.reshape(betas.shape), dg.reshape(dim))
+    return (
+        out.reshape(queries.shape), dq.reshape(queries.shape), dk.reshape(keys.shape), dv.reshape(values.shape), db.reshape(betas.shape), dg.reshape(dim),
+    )
 
 
 def solution(mesh):

time: 93.5 us -> 70.4 us (0.75)
  Pallas kernels: 85.4 us -> 62.8 us
    pallas_call x1, Pallas kernels: 85.4 us -> 62.8 us  [local(): pl.pallas_call(kernel, out_shape=(jax.ShapeDtypeStruct((tok * heads, dim)...]
where the time goes in v2:
time: 70.4 us; the launch traced here: 70.1 us
  Pallas kernels  62.8 us (89%)
  local copies, waits for them, and re-layouts  6.68 us (9%)
    pallas_call x1, Pallas kernels, local(): pl.pallas_call(kernel, out_shape=(jax.ShapeDtypeStruct((tok * heads, dim)...  62.8 us
    unnamed x19, local copies, waits for them, and re-layouts  6.68 us

profile of v2, /device:TPU:32, one launch (start us, length us, event | category | flops | bytes accessed | tf_op | source)
XLA Modules:
  0.0 70.1 jit_solution(14483150821007992)
XLA Ops:
  0.6 0.0 copy-start.4
  0.6 0.7 copy-done.4
  1.3 0.8 %copy.12 = f32[128,2,4]{2,1,0:T(2,128)} copy(f32[128,2,4]{0,2,1:T(4,128)S(1)} %copy-done.4) | data formatting | bytes 8192 | tf_op args[3]
  2.1 62.8 %delta_product.1 = (bf16[512,128]{1,0:T(8,128)(2,1)}, bf16[512,128]{1,0:T(8,128)(2,1)}, bf16[1024,128]{1,0:T(8,128)(2,1)}, bf16[1024,128]{1,0:T(8,128)(2,1)}, f32[256,4]{1,0:T(8,128)}, /*index=5*/f32[1,128]{1,0:T(1,128)}) custom-call(bf16[512,128]{1,0:T(8,128)(2,1)} %bitcast.17, bf16[1024,128]{1,0:T(8,128)(2,1)} %bitcast.13, bf16[1024,128]{1,0:T(8,128)(2,1)} %bitcast.14, ...), custom_call_target="tpu_custom_call" | custom-call | tf_op jit(solution)/shard_map/delta_product/pallas_call | solution.py:539
  64.9 0.0 copy-start.3
  64.9 0.0 copy-start.2
  64.9 1.6 %copy.13 = f32[128,2,4]{0,2,1:T(4,128)} copy(f32[128,2,4]{2,1,0:T(2,128)} %bitcast.21) | data formatting | bytes 8192
  66.5 0.0 copy-done.3
  66.5 0.0 copy-start.1
  66.5 0.7 copy.19
  67.2 0.0 copy-done.2
  67.2 0.7 copy.20
  67.8 0.0 copy-done.1
  67.8 0.0 copy-start
  67.8 0.7 %copy.21 = bf16[128,2,4,128]{3,2,1,0:T(4,128)(2,1)} copy(bf16[128,2,4,128]{3,2,1,0:T(4,128)(2,1)S(1)} %bitcast.16) | data formatting | bytes 524288
  68.5 0.3 copy-done
  68.9 0.0 copy-start.5
  68.9 0.7 %copy.22 = bf16[128,2,4,128]{3,2,1,0:T(4,128)(2,1)} copy(bf16[128,2,4,128]{3,2,1,0:T(4,128)(2,1)S(1)} %bitcast.15) | data formatting | bytes 524288
  69.6 0.0 copy-done.5
  69.6 0.5 copy.23
Async XLA Ops:
  0.6 0.7 copy-start.4
  64.9 1.6 %copy-start.3 = (bf16[512,128]{1,0:T(8,128)(2,1)S(1)}, bf16[512,128]{1,0:T(8,128)(2,1)}, u32[]{:S(2)}) copy-start(bf16[512,128]{1,0:T(8,128)(2,1)} %get-tuple-element.12) | copy-start | bytes 393220
  64.9 2.3 %copy-start.2 = (bf16[512,128]{1,0:T(8,128)(2,1)S(1)}, bf16[512,128]{1,0:T(8,128)(2,1)}, u32[]{:S(2)}) copy-start(bf16[512,128]{1,0:T(8,128)(2,1)} %get-tuple-element.13) | copy-start | bytes 393220
  66.5 1.3 %copy-start.1 = (bf16[1024,128]{1,0:T(8,128)(2,1)S(1)}, bf16[1024,128]{1,0:T(8,128)(2,1)}, u32[]{:S(2)}) copy-start(bf16[1024,128]{1,0:T(8,128)(2,1)} %get-tuple-element.14) | copy-start | bytes 786436
  67.8 1.0 %copy-start = (bf16[1024,128]{1,0:T(8,128)(2,1)S(1)}, bf16[1024,128]{1,0:T(8,128)(2,1)}, u32[]{:S(2)}) copy-start(bf16[1024,128]{1,0:T(8,128)(2,1)} %get-tuple-element.15) | copy-start | bytes 786436
  68.9 0.7 %copy-start.5 = (f32[1,128]{1,0:T(1,128)S(1)}, f32[1,128]{1,0:T(1,128)}, u32[]{:S(2)}) copy-start(f32[1,128]{1,0:T(1,128)} %get-tuple-element.17) | copy-start | bytes 1540

commit v3 on v2

--- a/solution.py
+++ b/solution.py
@@ -48,10 +48,11 @@
 
 
 def kernel(
-    q_ref, k_ref, v_ref, b_ref, g_ref, do_ref,
+    q_hbm, k_hbm, v_hbm, b_hbm, g_hbm, do_hbm,
     out_ref, dq_ref, dk_ref, dv_ref, db_ref, dg_ref,
+    q_ref, k_ref, v_ref, bt_ref, g_ref, do_ref, b_ref, db_s, in_sem,
     ku_s, qu_s, vf_s, dof_s, rk_s, rq_s, low_s, n_s, nt_s, nk_s, wu_s, sct_s, r_s, rt_s, ol_s, p_s, adj_s,
-    g0_s, dk1_s, of_s, dq_s, dk_s, dvf_s,
+    g0_s, dk1_s, of_s, dq_s, dk_s, dvf_s, dv_s,
     ab_s, pair_s, comp_s, own_s, phi_s, beta_s, zab_s, za_s, sout_s, sin_s, s1_s,
     aown_s, phi0_s, theta_s, psi_s, c_s, cpair_s, cc_s, cown_s, crow_s, zc_s, gam_s, dsend_s, dout_s, d0_s,
     gpart_s, grow_s, gz_s, gx_s, gsum_s,
@@ -59,6 +60,7 @@
     gsend_sem, grow_sem, gz_sem, gx_sem,
 ):
     steps, heads = b_ref.shape
+    per = steps // (q_ref.shape[0] // heads)
     tok = q_ref.shape[0] // heads
     dim = q_ref.shape[1]
     seq = lax.axis_index("seq")
@@ -91,6 +93,15 @@
         )
         count += 1
 
+    loads = [
+        pltpu.make_async_copy(src, dst, in_sem.at[n])
+        for n, (src, dst) in enumerate([
+            (k_hbm, k_ref), (b_hbm, bt_ref), (v_hbm, v_ref), (q_hbm, q_ref), (do_hbm, do_ref), (g_hbm, g_ref)
+        ])
+    ]
+    for load in loads:
+        load.start()
+
     def remote(src, dst, ssem, rsem, target):
         return pltpu.make_async_remote_copy(
             src_ref=src, dst_ref=dst, send_sem=ssem, recv_sem=rsem, device_id=target, device_id_type=MESH
@@ -115,6 +126,11 @@
             za_s[dlt - 1] = jnp.zeros((dim, dim), F32)
             zc_s[dlt - 1] = jnp.zeros((dim, dim), F32)
 
+    for load in loads:
+        load.wait()
+    turned = bt_ref[...].T
+    for j in range(per):
+        b_ref[pl.ds(j, tok, stride=per), :] = turned[:, j * heads:(j + 1) * heads]
     q = q_ref[...].astype(F32)
     k = k_ref[...].astype(F32)
     rq = lax.rsqrt(jnp.sum(q * q, axis=-1, keepdims=True) + EPS)
@@ -438,20 +454,23 @@
     lane = lax.broadcasted_iota(jnp.int32, (steps, heads), 1)
     db_all = jnp.zeros((steps, heads), F32)
     for h in range(heads):
-        p = p_s[h]
+        gm = g0_s[h] + mm(nk_s[h], dout_s[h])
         b = b_ref[:, h:h + 1]
-        d_out = dout_s[h]
-        gm = g0_s[h] + mm(nk_s[h], d_out)
         dv = b * gm
+        dv_s[h] = dv
         dvf_s[pl.ds(h, steps, stride=heads), :] = dv
-        db = jnp.sum(gm * p, axis=-1, keepdims=True) / b
+        db = jnp.sum(gm * p_s[h], axis=-1, keepdims=True) / b
         db_all = db_all + jnp.where(lane == h, db, 0.0)
-        hm = jnp.where(col_i < row_i, mm(dv, p, 1, 1), 0.0)
+    db_s[...] = db_all
+    for h in range(heads):
+        hm = jnp.where(col_i < row_i, mm(dv_s[h], p_s[h], 1, 1), 0.0)
+        low_s[h] = hm + hm.T
+    for h in range(heads):
         dk = dk1_s[h] + mm(
-            jnp.concatenate([p, dv], axis=1), jnp.concatenate([d_out, -sin_s[h]], axis=1), 1, 1
-        ) - mm(hm + hm.T, of_head(ku_s, h, steps))
+            jnp.concatenate([p_s[h], dv_s[h]], axis=1), jnp.concatenate([dout_s[h], -sin_s[h]], axis=1), 1, 1
+        ) - mm(low_s[h], of_head(ku_s, h, steps))
         dk_s[pl.ds(h, steps, stride=heads), :] = dk
-    db_ref[...] = db_all
+    db_ref[...] = jnp.concatenate([db_s[pl.ds(j, tok, stride=per), :] for j in range(per)], axis=1).T
     out_ref[...] = of_s[...].astype(BF16)
     dq_ref[...] = unit_pullback(dq_s[...], qu_s[...], rq_s[...]).astype(BF16)
     dk_ref[...] = unit_pullback(dk_s[...], ku_s[...], rk_s[...]).astype(BF16)
@@ -514,17 +533,21 @@
 
 def local(queries, keys, values, betas, gain, out_grad):
     tok, heads, dim = queries.shape
-    steps = tok * keys.shape[1]
+    per = keys.shape[1]
+    steps = tok * per
     f = lambda *s: pltpu.VMEM(s, F32)
     dma = pltpu.SemaphoreType.DMA
     vmem = pl.BlockSpec(memory_space=pltpu.VMEM)
+    b16 = lambda *sh: pltpu.VMEM(sh, BF16)
     scratch = [
+        b16(tok * heads, dim), b16(steps * heads, dim), b16(steps * heads, dim), f(per * heads, tok), f(1, dim),
+        b16(tok * heads, dim), f(steps, heads), f(steps, heads), dma((6,)),
         f(steps * heads, dim), f(tok * heads, dim), f(steps * heads, dim), f(tok * heads, dim),
         f(steps * heads, 1), f(tok * heads, 1), f(heads, steps, steps), f(heads, steps, steps),
         f(heads, steps, steps), f(heads, steps, dim), f(heads, steps, 2 * dim), f(heads, steps, tok),
         f(heads, tok, dim), f(heads, dim, tok), f(heads, tok, dim), f(heads, steps, dim), f(heads, tok, dim),
         f(heads, steps, dim), f(heads, steps, dim), f(tok * heads, dim), f(tok * heads, dim),
-        f(steps * heads, dim), f(steps * heads, dim),
+        f(steps * heads, dim), f(steps * heads, dim), f(heads, steps, dim),
         f(heads, 2, dim, dim), f(2, 2, dim, dim), f(2, 2, dim, dim), f(NY, 2, dim, dim),
         f(NY, dim, dim), f(NY, dim, dim), f(NZ - 1, 2, dim, dim), f(NZ - 1, dim, dim),
         f(NY, dim, dim), f(heads, dim, dim), f(heads, dim, dim),
@@ -543,28 +566,46 @@
             jax.ShapeDtypeStruct((tok * heads, dim), BF16),
             jax.ShapeDtypeStruct((steps * heads, dim), BF16),
             jax.ShapeDtypeStruct((steps * heads, dim), BF16),
-            jax.ShapeDtypeStruct((steps, heads), F32),
+            jax.ShapeDtypeStruct((per * heads, tok), F32),
             jax.ShapeDtypeStruct((1, dim), F32),
         ),
-        in_specs=[vmem] * 6,
+        in_specs=[pl.BlockSpec(memory_space=pltpu.HBM)] * 6,
         out_specs=(vmem,) * 6,
         scratch_shapes=scratch,
         compiler_params=pltpu.CompilerParams(
-            collective_id=0, has_side_effects=True, vmem_limit_bytes=60 * 1024 * 1024
+            collective_id=0, has_side_effects=True, vmem_limit_bytes=32 * 1024 * 1024
         ),
         name="delta_product",
     )(
         queries.reshape(tok * heads, dim),
         keys.reshape(steps * heads, dim),
         values.reshape(steps * heads, dim),
-        betas.reshape(steps, heads),
+        betas.transpose(1, 2, 0).reshape(per * heads, tok),
         gain.reshape(1, dim),
         out_grad.reshape(tok * heads, dim),
     )
-    out, dq, dk, dv, db, dg = outs
+    out, dq, dk, dv, db, dg = pl.pallas_call(
+        store,
+        out_shape=tuple(jax.ShapeDtypeStruct(a.shape, a.dtype) for a in outs),
+        in_specs=[vmem] * 6,
+        out_specs=(pl.BlockSpec(memory_space=pl.ANY),) * 6,
+        scratch_shapes=[dma((6,))],
+        compiler_params=pltpu.CompilerParams(vmem_limit_bytes=4 * 1024 * 1024),
+        name="store",
+    )(*outs)
     return (
-        out.reshape(queries.shape), dq.reshape(queries.shape), dk.reshape(keys.shape), dv.reshape(values.shape), db.reshape(betas.shape), dg.reshape(dim),
+        out.reshape(queries.shape), dq.reshape(queries.shape), dk.reshape(keys.shape), dv.reshape(values.shape),
+        db.reshape(per, heads, tok).transpose(2, 0, 1), dg.reshape(dim),
     )
+
+
+def store(*refs):
+    sem = refs[-1]
+    copies = [pltpu.make_async_copy(refs[n], refs[6 + n], sem.at[n]) for n in range(6)]
+    for copy in copies:
+        copy.start()
+    for copy in copies:
+        copy.wait()
 
 
 def solution(mesh):

time: 70.4 us -> 67.1 us (0.953)
  local copies, waits for them, and re-layouts: 6.68 us -> 4.38 us
  Pallas kernels: 62.8 us -> 61.6 us
    unnamed x19 -> x12, local copies, waits for them, and re-layouts: 6.68 us -> 4.38 us
    pallas_call x1, Pallas kernels: 62.8 us -> 60.7 us  [local(): pl.pallas_call(kernel, out_shape=(jax.ShapeDtypeStruct((tok * heads, dim)...]
    pallas_call x0 -> x1, Pallas kernels: none -> 0.93 us  [local(): pl.pallas_call(store, out_shape=tuple((jax.ShapeDtypeStruct(a.shape, a.dt...]
where the time goes in v3:
time: 67.1 us; the launch traced here: 66.8 us
  Pallas kernels  61.6 us (92%)
  local copies, waits for them, and re-layouts  4.38 us (7%)
  between operations  0.84 us (1%)
    pallas_call x1, Pallas kernels, local(): pl.pallas_call(kernel, out_shape=(jax.ShapeDtypeStruct((tok * heads, dim)...  60.7 us
    unnamed x12, local copies, waits for them, and re-layouts  4.38 us

profile of v3, /device:TPU:32, one launch (start us, length us, event | category | flops | bytes accessed | tf_op | source)
XLA Modules:
  0.0 66.8 jit_solution(4574908833068615429)
XLA Ops:
  0.6 0.0 copy-start.4
  0.6 0.0 copy-start.5
  0.7 0.7 copy-done.4
  1.3 0.0 copy-done.5
  1.3 0.0 copy-start
  1.3 0.9 %copy-done = bf16[128,2,4,128]{3,2,1,0:T(4,128)(2,1)S(1)} copy-done((bf16[128,2,4,128]{3,2,1,0:T(4,128)(2,1)S(1)}, bf16[128,2,4,128]{3,2,1,0:T(4,128)(2,1)}, u32[]{:S(2)}) %copy-start) | copy-done | bytes 262168
  2.3 0.0 copy-start.1
  2.3 0.9 %copy-done.1 = bf16[128,2,4,128]{3,2,1,0:T(4,128)(2,1)S(1)} copy-done((bf16[128,2,4,128]{3,2,1,0:T(4,128)(2,1)S(1)}, bf16[128,2,4,128]{3,2,1,0:T(4,128)(2,1)}, u32[]{:S(2)}) %copy-start.1) | copy-done | bytes 262168
  3.2 0.0 copy-start.2
  3.2 0.9 %copy-done.2 = bf16[128,4,128]{2,1,0:T(4,128)(2,1)S(1)} copy-done((bf16[128,4,128]{2,1,0:T(4,128)(2,1)S(1)}, bf16[128,4,128]{2,1,0:T(4,128)(2,1)}, u32[]{:S(2)}) %copy-start.2) | copy-done | bytes 131096
  4.1 0.0 copy-start.3
  4.1 0.9 %copy-done.3 = bf16[128,4,128]{2,1,0:T(4,128)(2,1)S(1)} copy-done((bf16[128,4,128]{2,1,0:T(4,128)(2,1)S(1)}, bf16[128,4,128]{2,1,0:T(4,128)(2,1)}, u32[]{:S(2)}) %copy-start.3) | copy-done | bytes 131096
  5.0 60.7 %delta_product.1 = (bf16[512,128]{1,0:T(8,128)(2,1)S(1)}, bf16[512,128]{1,0:T(8,128)(2,1)S(1)}, bf16[1024,128]{1,0:T(8,128)(2,1)S(1)}, bf16[1024,128]{1,0:T(8,12...) custom-call(bf16[512,128]{1,0:T(8,128)(2,1)S(1)} %bitcast.18, bf16[1024,128]{1,0:T(8,128)(2,1)S(1)} %bitcast.16, ...), custom_call_target="tpu_custom_call" | custom-call | tf_op jit(solution)/shard_map/delta_product/pallas_call | solution.py:562
  65.7 0.9 %store.1 = (bf16[512,128]{1,0:T(8,128)(2,1)}, bf16[512,128]{1,0:T(8,128)(2,1)}, bf16[1024,128]{1,0:T(8,128)(2,1)}, bf16[1024,128]{1,0:T(8,128)(2,1)}, f32[8,128]{1,0:T(8,128)}, /*index=5*/f32[1,128]{1,0:T(1,128)}) custom-call(bf16[512,128]{1,0:T(8,128)(2,1)S(1)} %get-tuple-element.18.refs_0_, bf16[512,128]{1,0:T(8,128)(2,1)S(1)} %get-tuple-element.19.refs_1_, ...), custom_call_target="tpu_custom_call" | custom-call | tf_op jit(solution)/shard_map/store/pallas_call | solution.py:587
Async XLA Ops:
  0.6 0.7 %copy-start.4 = (f32[128,2,4]{0,2,1:T(4,128)S(1)}, f32[128,2,4]{0,2,1:T(4,128)}, u32[]{:S(2)}) copy-start(f32[128,2,4]{0,2,1:T(4,128)} %param.9) | copy-start | bytes 12292
  0.6 0.7 %copy-start.5 = (f32[128]{0:T(128)S(1)}, f32[128]{0:T(128)}, u32[]{:S(2)}) copy-start(f32[128]{0:T(128)} %param.10) | copy-start | bytes 1540
  1.3 1.0 %copy-start = (bf16[128,2,4,128]{3,2,1,0:T(4,128)(2,1)S(1)}, bf16[128,2,4,128]{3,2,1,0:T(4,128)(2,1)}, u32[]{:S(2)}) copy-start(bf16[128,2,4,128]{3,2,1,0:T(4,128)(2,1)} %param.7) | copy-start | bytes 786436
  2.3 0.9 %copy-start.1 = (bf16[128,2,4,128]{3,2,1,0:T(4,128)(2,1)S(1)}, bf16[128,2,4,128]{3,2,1,0:T(4,128)(2,1)}, u32[]{:S(2)}) copy-start(bf16[128,2,4,128]{3,2,1,0:T(4,128)(2,1)} %param.8) | copy-start | bytes 786436
  3.2 0.9 %copy-start.2 = (bf16[128,4,128]{2,1,0:T(4,128)(2,1)S(1)}, bf16[128,4,128]{2,1,0:T(4,128)(2,1)}, u32[]{:S(2)}) copy-start(bf16[128,4,128]{2,1,0:T(4,128)(2,1)} %param.6) | copy-start | bytes 393220
  4.1 0.9 %copy-start.3 = (bf16[128,4,128]{2,1,0:T(4,128)(2,1)S(1)}, bf16[128,4,128]{2,1,0:T(4,128)(2,1)}, u32[]{:S(2)}) copy-start(bf16[128,4,128]{2,1,0:T(4,128)(2,1)} %param.11) | copy-start | bytes 393220

commit v4 on v3

--- a/solution.py
+++ b/solution.py
@@ -13,6 +13,7 @@
 MESH = pl.DeviceIdType.MESH
 NY = 4
 NZ = 8
+NG = 4
 NC = 2
 
 
@@ -55,7 +56,7 @@
     g0_s, dk1_s, of_s, dq_s, dk_s, dvf_s, dv_s,
     ab_s, pair_s, comp_s, own_s, phi_s, beta_s, zab_s, za_s, sout_s, sin_s, s1_s,
     aown_s, phi0_s, theta_s, psi_s, c_s, cpair_s, cc_s, cown_s, crow_s, zc_s, gam_s, dsend_s, dout_s, d0_s,
-    gpart_s, grow_s, gz_s, gx_s, gsum_s,
+    gpart_s, grow_s, gz_s, gx_s, gsum_s, x_s, middle_s, mid_s, mid_sem,
     send_sem, pair_sem, own_sem, zab_sem, za_sem, sin_sem, aown_sem, cpair_sem, cown_sem, zc_sem, dout_sem,
     gsend_sem, grow_sem, gz_sem, gx_sem,
 ):
@@ -110,6 +111,21 @@
     def arrived(dst, rsem):
         pltpu.make_async_copy(dst, dst, rsem).wait()
 
+    group = z // NG
+    rank = z % NG
+
+    def zab_copy(dlt):
+        return remote(
+            own_s.at[0], zab_s.at[rank], send_sem.at[4 + dlt], zab_sem.at[rank], dev(z + dlt, y, 1)
+        )
+
+    def zback_copy():
+        return remote(own_s.at[0], zab_s.at[rank], send_sem.at[8], zab_sem.at[rank], dev(0, y, 1))
+
+    def middle_copy(n):
+        to = jnp.where(rank == 0, NZ - 1 - n, NG + n)
+        return remote(middle_s, mid_s, send_sem.at[9 + n], mid_sem, dev(to, y, 1))
+
     row_i, col_i = iotas(steps, steps)
     tok_i, step_i = iotas(tok, steps)
     visible = step_i <= 2 * tok_i + 1
@@ -117,10 +133,6 @@
     eye_dim = eye[:dim, :dim]
 
     for dlt in range(1, NZ):
-        @pl.when(z < dlt)
-        def _():
-            zab_s[dlt - 1] = jnp.zeros((2, dim, dim), F32)
-
         @pl.when(z + dlt >= NZ)
         def _():
             za_s[dlt - 1] = jnp.zeros((dim, dim), F32)
@@ -229,6 +241,8 @@
             dq_s[pl.ds(h, tok, stride=heads), :] = dq
             dk1_s[h] = mm(m_do.T, of_head(qu_s, h, tok))
             g0_s[h] = mm(nt_s[h], mm(sct_s[h], adj))
+        out_ref[...] = of_s[...].astype(BF16)
+        dq_ref[...] = unit_pullback(dq_s[...], qu_s[...], rq_s[...]).astype(BF16)
 
     pl.semaphore_wait(barrier, count)
 
@@ -276,13 +290,68 @@
         comp_row = own_s.at[0]
         comp_row[0] = x[:, :dim]
         comp_row[1] = x[:, dim:]
-        for dlt in range(NZ - 1, 0, -1):
-            @pl.when(z + dlt < NZ)
-            def _():
-                remote(
-                    own_s.at[0], zab_s.at[dlt - 1], send_sem.at[4 + dlt], zab_sem.at[dlt - 1],
-                    dev(z + dlt, y, 1),
-                ).start()
+        for dlt in range(NG - 1, 0, -1):
+            @pl.when(rank + dlt < NG)
+            def _():
+                zab_copy(dlt).start()
+
+        @pl.when((group == 0) & (rank > 0))
+        def _():
+            zback_copy().start()
+
+        for i in range(1, NY):
+            remote(own_s.at[i, 0], aown_s.at[i], send_sem.at[20 + i], aown_sem.at[i], low_core).start()
+            remote(phi_s.at[i - 1], phi0_s.at[i], send_sem.at[24 + i], aown_sem.at[NY + i], low_core).start()
+        fill_forward()
+
+        @pl.when(rank == 0)
+        def _():
+            x_s[:, :dim] = eye_dim
+            x_s[:, dim:] = jnp.zeros((dim, dim), F32)
+
+        for i in range(NG - 1):
+            @pl.when(rank > i)
+            def _():
+                arrived(zab_s.at[i], zab_sem.at[i])
+                if i == 0:
+                    x_s[:, :dim] = zab_s[0, 0]
+                    x_s[:, dim:] = zab_s[0, 1]
+                else:
+                    nxt = mm(zab_s[i, 0], x_s[...])
+                    x_s[:, :dim] = nxt[:, :dim]
+                    x_s[:, dim:] = nxt[:, dim:] + zab_s[i, 1]
+
+        @pl.when((group == 0) & (rank == NG - 1))
+        def _():
+            middle_s[...] = mm(own_s[0, 0], x_s[:, dim:]) + own_s[0, 1]
+            for n in range(2):
+                middle_copy(n).start()
+
+        @pl.when((group == 0) & (rank == 0))
+        def _():
+            state = own_s[0, 1]
+            for i in range(1, NG):
+                arrived(zab_s.at[i], zab_sem.at[i])
+                state = mm(zab_s[i, 0], state) + zab_s[i, 1]
+            middle_s[...] = state
+            for n in range(2):
+                middle_copy(n).start()
+
+        sout_s[0] = x_s[:, dim:]
+        later = mm(jnp.concatenate([phi_s[i] for i in range(NY - 1)], axis=0), x_s[...])
+        for i in range(1, NY):
+            sout_s[i] = later[(i - 1) * dim:i * dim, dim:] + beta_s[i - 1]
+
+        @pl.when(group == 1)
+        def _():
+            arrived(mid_s, mid_sem)
+            stack = jnp.concatenate([x_s[:, :dim], later[:, :dim]], axis=0)
+            more = mm(stack, mid_s[...])
+            for i in range(NY):
+                sout_s[i] = sout_s[i] + more[i * dim:(i + 1) * dim]
+
+        for i in range(NY):
+            remote(sout_s.at[i], sin_s.at[y], send_sem.at[28 + i], sin_sem.at[y], dev(z, i, 0)).start()
         for dlt in range(1, NZ):
             @pl.when(z >= dlt)
             def _():
@@ -290,26 +359,6 @@
                     phi_s.at[NY - 1], za_s.at[dlt - 1], send_sem.at[12 + dlt], za_sem.at[dlt - 1],
                     dev(z - dlt, y, 0),
                 ).start()
-        for i in range(1, NY):
-            remote(own_s.at[i, 0], aown_s.at[i], send_sem.at[20 + i], aown_sem.at[i], low_core).start()
-            remote(phi_s.at[i - 1], phi0_s.at[i], send_sem.at[24 + i], aown_sem.at[NY + i], low_core).start()
-        fill_forward()
-        state = jnp.zeros((dim, dim), F32)
-        for dlt in range(NZ - 1, 0, -1):
-            @pl.when(z >= dlt)
-            def _():
-                arrived(zab_s.at[dlt - 1], zab_sem.at[dlt - 1])
-
-            if dlt == NZ - 1:
-                state = zab_s[dlt - 1, 1]
-            else:
-                state = mm(zab_s[dlt - 1, 0], state) + zab_s[dlt - 1, 1]
-        sout_s[0] = state
-        later = mm(jnp.concatenate([phi_s[i] for i in range(NY - 1)], axis=0), state)
-        for i in range(1, NY):
-            sout_s[i] = later[(i - 1) * dim:i * dim] + beta_s[i - 1]
-        for i in range(NY):
-            remote(sout_s.at[i], sin_s.at[y], send_sem.at[28 + i], sin_sem.at[y], dev(z, i, 0)).start()
         for h in range(heads):
             arrived(sin_s.at[h], sin_sem.at[h])
 
@@ -322,18 +371,6 @@
         psi_s[NY - 2] = aown_s[NY - 1]
         for i in range(NY - 3, -1, -1):
             psi_s[i] = mm(psi_s[i + 1], aown_s[i + 1])
-        theta_s[0] = eye_dim
-        for dlt in range(1, NZ - 1):
-            @pl.when(z + dlt < NZ)
-            def _():
-                arrived(za_s.at[dlt - 1], za_sem.at[dlt - 1])
-
-            theta_s[dlt] = za_s[0] if dlt == 1 else mm(za_s[dlt - 1], theta_s[dlt - 1])
-
-        @pl.when(z + NZ - 1 < NZ)
-        def _():
-            arrived(za_s.at[NZ - 2], za_sem.at[NZ - 2])
-
         for h in range(heads):
             arrived(sin_s.at[h], sin_sem.at[h])
             s1_s[h] = mm(ab_s[h, 0], sin_s[h]) + ab_s[h, 1]
@@ -342,19 +379,20 @@
     gain = g_ref[...]
     gain_part = jnp.zeros((1, dim), F32)
     for h in range(heads):
-        state = sin_s[h]
-        both = mm(jnp.concatenate([r_s[h], wu_s[h, :, :dim]], axis=0), state)
-        o = ol_s[h] + both[:tok]
+        both = mm(jnp.concatenate([r_s[h], wu_s[h, :, :dim]], axis=0), sin_s[h])
+        ol_s[h] = ol_s[h] + both[:tok]
         p_s[h] = wu_s[h, :, dim:] - both[tok:]
+    for h in range(heads):
+        o = ol_s[h]
         inv_rms = lax.rsqrt(jnp.mean(o * o, axis=-1, keepdims=True) + EPS)
         normal = o * inv_rms
         grad = of_head(dof_s, h, tok)
         of_s[pl.ds(h, tok, stride=heads), :] = gain * normal
         gain_part = gain_part + jnp.sum(grad * normal, axis=0, keepdims=True)
         scaled = grad * gain
-        adj = inv_rms * (scaled - normal * jnp.mean(scaled * normal, axis=-1, keepdims=True))
-        adj_s[h] = adj
-        c_s[h] = mm(rt_s[h], adj)
+        adj_s[h] = inv_rms * (scaled - normal * jnp.mean(scaled * normal, axis=-1, keepdims=True))
+    for h in range(heads):
+        c_s[h] = mm(rt_s[h], adj_s[h])
 
         @pl.when(c == 1)
         def _():
@@ -420,6 +458,17 @@
             gam_s[i] = mm(aown_s[i + 1], gam_s[i + 1], 0, 0) + cown_s[i + 1]
         gain_along_z()
         fill_backward()
+        for dlt in range(1, NZ - 1):
+            @pl.when(z + dlt < NZ)
+            def _():
+                arrived(za_s.at[dlt - 1], za_sem.at[dlt - 1])
+
+            theta_s[dlt] = za_s[0] if dlt == 1 else mm(za_s[dlt - 1], theta_s[dlt - 1])
+
+        @pl.when(z + NZ - 1 < NZ)
+        def _():
+            arrived(za_s.at[NZ - 2], za_sem.at[NZ - 2])
+
         for dlt in range(NZ - 1, 0, -1):
             @pl.when(z + dlt < NZ)
             def _():
@@ -471,8 +520,6 @@
         ) - mm(low_s[h], of_head(ku_s, h, steps))
         dk_s[pl.ds(h, steps, stride=heads), :] = dk
     db_ref[...] = jnp.concatenate([db_s[pl.ds(j, tok, stride=per), :] for j in range(per)], axis=1).T
-    out_ref[...] = of_s[...].astype(BF16)
-    dq_ref[...] = unit_pullback(dq_s[...], qu_s[...], rq_s[...]).astype(BF16)
     dk_ref[...] = unit_pullback(dk_s[...], ku_s[...], rk_s[...]).astype(BF16)
     dv_ref[...] = dvf_s[...].astype(BF16)
 
@@ -493,11 +540,21 @@
 
     @pl.when(c == 1)
     def _():
+        for dlt in range(1, NG):
+            @pl.when(rank + dlt < NG)
+            def _():
+                zab_copy(dlt).wait_send()
+
+        @pl.when((group == 0) & (rank > 0))
+        def _():
+            zback_copy().wait_send()
+
+        @pl.when((z == 0) | (z == NG - 1))
+        def _():
+            for n in range(2):
+                middle_copy(n).wait_send()
+
         for dlt in range(1, NZ):
-            @pl.when(z + dlt < NZ)
-            def _():
-                left(own_s.at[0], send_sem.at[4 + dlt])
-
             @pl.when(z >= dlt)
             def _():
                 left(phi_s.at[NY - 1], send_sem.at[12 + dlt])
@@ -549,13 +606,14 @@
         f(heads, steps, dim), f(heads, steps, dim), f(tok * heads, dim), f(tok * heads, dim),
         f(steps * heads, dim), f(steps * heads, dim), f(heads, steps, dim),
         f(heads, 2, dim, dim), f(2, 2, dim, dim), f(2, 2, dim, dim), f(NY, 2, dim, dim),
-        f(NY, dim, dim), f(NY, dim, dim), f(NZ - 1, 2, dim, dim), f(NZ - 1, dim, dim),
+        f(NY, dim, dim), f(NY, dim, dim), f(NG, 2, dim, dim), f(NZ - 1, dim, dim),
         f(NY, dim, dim), f(heads, dim, dim), f(heads, dim, dim),
         f(NY, dim, dim), f(NY, dim, dim), f(NZ - 1, dim, dim), f(NY - 1, dim, dim), f(heads, dim, dim),
         f(heads, dim, dim), f(heads, dim, dim), f(NY, dim, dim), f(dim, dim), f(NZ - 1, dim, dim),
         f(NY - 1, dim, dim), f(NY, dim, dim), f(heads, dim, dim), f(heads, dim, dim),
         f(8, dim), f(NY * NC, 8, dim), f(NZ, 8, dim), f(4, 8, dim), f(2, 8, dim),
-        dma((40,)), dma((2,)), dma((NY,)), dma((NZ - 1,)), dma((NZ - 1,)), dma((heads,)), dma((2 * NY,)),
+        f(dim, 2 * dim), f(dim, dim), f(dim, dim), dma,
+        dma((40,)), dma((2,)), dma((NY,)), dma((NG,)), dma((NZ - 1,)), dma((heads,)), dma((2 * NY,)),
         dma((heads,)), dma((NY,)), dma((NZ - 1,)), dma((heads,)),
         dma((24,)), dma((NY * NC - 1,)), dma((NZ - 1,)), dma((3,)),
     ]
@@ -576,14 +634,17 @@
             collective_id=0, has_side_effects=True, vmem_limit_bytes=32 * 1024 * 1024
         ),
         name="delta_product",
-    )(
-        queries.reshape(tok * heads, dim),
-        keys.reshape(steps * heads, dim),
-        values.reshape(steps * heads, dim),
-        betas.transpose(1, 2, 0).reshape(per * heads, tok),
-        gain.reshape(1, dim),
-        out_grad.reshape(tok * heads, dim),
-    )
+    )(*[
+        pltpu.with_memory_space_constraint(a, pltpu.HBM)
+        for a in (
+            queries.reshape(tok * heads, dim),
+            keys.reshape(steps * heads, dim),
+            values.reshape(steps * heads, dim),
+            betas.transpose(1, 2, 0).reshape(per * heads, tok),
+            gain.reshape(1, dim),
+            out_grad.reshape(tok * heads, dim),
+        )
+    ])
     out, dq, dk, dv, db, dg = pl.pallas_call(
         store,
         out_shape=tuple(jax.ShapeDtypeStruct(a.shape, a.dtype) for a in outs),

time: 67.1 us -> 59.9 us (0.89)
  local copies, waits for them, and re-layouts: 4.38 us -> 0 us
  Pallas kernels: 61.6 us -> 58.2 us
    unnamed x12 -> x0, local copies, waits for them, and re-layouts: 4.38 us -> none
    pallas_call x1, Pallas kernels: 60.7 us -> 57.3 us  [local(): pl.pallas_call(kernel, out_shape=(jax.ShapeDtypeStruct((tok * heads, dim)...]
where the time goes in v4:
time: 59.9 us; the launch traced here: 59 us
  Pallas kernels  58.2 us (97%)
  between operations  0.82 us (1%)
    pallas_call x1, Pallas kernels, local(): pl.pallas_call(kernel, out_shape=(jax.ShapeDtypeStruct((tok * heads, dim)...  57.3 us

profile of v4, /device:TPU:32, one launch (start us, length us, event | category | flops | bytes accessed | tf_op | source)
XLA Modules:
  0.0 59.0 jit_solution(8237623378031895390)
XLA Ops:
  0.6 57.3 %delta_product.1 = (bf16[512,128]{1,0:T(8,128)(2,1)S(1)}, bf16[512,128]{1,0:T(8,128)(2,1)S(1)}, bf16[1024,128]{1,0:T(8,128)(2,1)S(1)}, bf16[1024,128]{1,0:T(8,12...) custom-call(bf16[512,128]{1,0:T(8,128)(2,1)} %bitcast.18, bf16[1024,128]{1,0:T(8,128)(2,1)} %bitcast.16, ...), custom_call_target="tpu_custom_call" | custom-call | tf_op jit(solution)/shard_map/delta_product/pallas_call | solution.py:620
  57.9 0.9 %store.1 = (bf16[512,128]{1,0:T(8,128)(2,1)}, bf16[512,128]{1,0:T(8,128)(2,1)}, bf16[1024,128]{1,0:T(8,128)(2,1)}, bf16[1024,128]{1,0:T(8,128)(2,1)}, f32[8,128]{1,0:T(8,128)}, /*index=5*/f32[1,128]{1,0:T(1,128)}) custom-call(bf16[512,128]{1,0:T(8,128)(2,1)S(1)} %get-tuple-element.18.refs_0_, bf16[512,128]{1,0:T(8,128)(2,1)S(1)} %get-tuple-element.19.refs_1_, ...), custom_call_target="tpu_custom_call" | custom-call | tf_op jit(solution)/shard_map/store/pallas_call | solution.py:648

commit v5 on v4

--- a/solution.py
+++ b/solution.py
@@ -56,7 +56,7 @@
     g0_s, dk1_s, of_s, dq_s, dk_s, dvf_s, dv_s,
     ab_s, pair_s, comp_s, own_s, phi_s, beta_s, zab_s, za_s, sout_s, sin_s, s1_s,
     aown_s, phi0_s, theta_s, psi_s, c_s, cpair_s, cc_s, cown_s, crow_s, zc_s, gam_s, dsend_s, dout_s, d0_s,
-    gpart_s, grow_s, gz_s, gx_s, gsum_s, x_s, middle_s, mid_s, mid_sem,
+    gpart_s, grow_s, gz_s, gx_s, gsum_s, xa_s, xb_s, middle_s, mid_s, mid_sem,
     send_sem, pair_sem, own_sem, zab_sem, za_sem, sin_sem, aown_sem, cpair_sem, cown_sem, zc_sem, dout_sem,
     gsend_sem, grow_sem, gz_sem, gx_sem,
 ):
@@ -114,13 +114,46 @@
     group = z // NG
     rank = z % NG
 
-    def zab_copy(dlt):
+    near_first = [(y + d) % NY for d in (0, 1, 3, 2)]
+
+    def own_copy(j, part):
+        head = 2 * c + j
         return remote(
-            own_s.at[0], zab_s.at[rank], send_sem.at[4 + dlt], zab_sem.at[rank], dev(z + dlt, y, 1)
-        )
-
-    def zback_copy():
-        return remote(own_s.at[0], zab_s.at[rank], send_sem.at[8], zab_sem.at[rank], dev(0, y, 1))
+            comp_s.at[j, part], own_s.at[y, part], send_sem.at[2 + j if part == 0 else 45 + j],
+            own_sem.at[part * NY + y], dev(z, head, 1),
+        )
+
+    def own_here(j):
+        return (c == 1) & (y == 2 * c + j)
+
+    def own_start(j, part):
+        @pl.when(own_here(j))
+        def _():
+            pltpu.make_async_copy(
+                comp_s.at[j, part], own_s.at[y, part], own_sem.at[part * NY + y]
+            ).start()
+
+        @pl.when(jnp.logical_not(own_here(j)))
+        def _():
+            own_copy(j, part).start()
+
+    def zab_copy(dlt, part, back=False):
+        src = (beta_s if part else phi_s).at[NY - 1]
+        to = 0 if back else z + dlt
+        sem = (8, 44)[part] if back else (4, 40)[part] + dlt
+        return remote(
+            src, zab_s.at[rank, part], send_sem.at[sem], zab_sem.at[part * NG + rank], dev(to, y, 1)
+        )
+
+    def zab_each(part, act):
+        for dlt in range(NG - 1, 0, -1):
+            @pl.when((rank + dlt < NG) & ((z > 0) | (part == 1)))
+            def _():
+                act(zab_copy(dlt, part))
+
+        @pl.when((group == 0) & (rank > 0))
+        def _():
+            act(zab_copy(0, part, True))
 
     def middle_copy(n):
         to = jnp.where(rank == 0, NZ - 1 - n, NG + n)
@@ -263,94 +296,88 @@
         both = mm(second[0], jnp.concatenate([first[0], first[1]], axis=1))
         comp_s[j, 0] = both[:, :dim]
         comp_s[j, 1] = both[:, dim:] + second[1]
-        head = 2 * c + j
-        here = (c == 1) & (y == head)
-
-        @pl.when(here)
-        def _():
-            pltpu.make_async_copy(comp_s.at[j], own_s.at[y], own_sem.at[y]).start()
-
-        @pl.when(jnp.logical_not(here))
-        def _():
-            remote(comp_s.at[j], own_s.at[y], send_sem.at[2 + j], own_sem.at[y], dev(z, head, 1)).start()
+        own_start(j, 0)
+    for j in range(2):
+        own_start(j, 1)
 
     @pl.when(c == 1)
     def _():
         low_core = dev(z, y, 0)
-        arrived(own_s.at[0], own_sem.at[0])
-        x = jnp.concatenate([own_s[0, 0], own_s[0, 1]], axis=1)
-        phi_s[0] = x[:, :dim]
-        beta_s[0] = x[:, dim:]
-        for i in range(1, NY):
-            arrived(own_s.at[i], own_sem.at[i])
-            x = mm(own_s[i, 0], x)
-            x = jnp.concatenate([x[:, :dim], x[:, dim:] + own_s[i, 1]], axis=1)
-            phi_s[i] = x[:, :dim]
-            beta_s[i] = x[:, dim:]
-        comp_row = own_s.at[0]
-        comp_row[0] = x[:, :dim]
-        comp_row[1] = x[:, dim:]
-        for dlt in range(NG - 1, 0, -1):
-            @pl.when(rank + dlt < NG)
-            def _():
-                zab_copy(dlt).start()
-
-        @pl.when((group == 0) & (rank > 0))
-        def _():
-            zback_copy().start()
+        for i in range(NY):
+            arrived(own_s.at[i, 0], own_sem.at[i])
+            phi_s[i] = mm(own_s[i, 0], phi_s[i - 1]) if i else own_s[0, 0]
+        zab_each(0, lambda copy: copy.start())
+        for i in range(NY):
+            arrived(own_s.at[i, 1], own_sem.at[NY + i])
+            beta_s[i] = mm(own_s[i, 0], beta_s[i - 1]) + own_s[i, 1] if i else own_s[0, 1]
+        zab_each(1, lambda copy: copy.start())
 
         for i in range(1, NY):
             remote(own_s.at[i, 0], aown_s.at[i], send_sem.at[20 + i], aown_sem.at[i], low_core).start()
             remote(phi_s.at[i - 1], phi0_s.at[i], send_sem.at[24 + i], aown_sem.at[NY + i], low_core).start()
         fill_forward()
 
+        phis = jnp.concatenate([phi_s[i] for i in range(NY - 1)], axis=0)
+
+        @pl.when(group == 1)
+        def _():
+            @pl.when(rank == 0)
+            def _():
+                xa_s[0:dim] = eye_dim
+
+            for i in range(NG - 1):
+                @pl.when(rank > i)
+                def _():
+                    arrived(zab_s.at[i, 0], zab_sem.at[i])
+                    xa_s[0:dim] = mm(zab_s[i, 0], xa_s[0:dim]) if i else zab_s[0, 0]
+            xa_s[dim:] = mm(phis, xa_s[0:dim])
+
+        @pl.when(group == 0)
+        def _():
+            for i in range(1, NG):
+                @pl.when((rank > i) | (rank == 0))
+                def _():
+                    arrived(zab_s.at[i, 0], zab_sem.at[i])
+
         @pl.when(rank == 0)
         def _():
-            x_s[:, :dim] = eye_dim
-            x_s[:, dim:] = jnp.zeros((dim, dim), F32)
+            xb_s[...] = jnp.zeros((dim, dim), F32)
 
         for i in range(NG - 1):
             @pl.when(rank > i)
             def _():
-                arrived(zab_s.at[i], zab_sem.at[i])
-                if i == 0:
-                    x_s[:, :dim] = zab_s[0, 0]
-                    x_s[:, dim:] = zab_s[0, 1]
-                else:
-                    nxt = mm(zab_s[i, 0], x_s[...])
-                    x_s[:, :dim] = nxt[:, :dim]
-                    x_s[:, dim:] = nxt[:, dim:] + zab_s[i, 1]
+                arrived(zab_s.at[i, 1], zab_sem.at[NG + i])
+                xb_s[...] = mm(zab_s[i, 0], xb_s[...]) + zab_s[i, 1] if i else zab_s[0, 1]
 
         @pl.when((group == 0) & (rank == NG - 1))
         def _():
-            middle_s[...] = mm(own_s[0, 0], x_s[:, dim:]) + own_s[0, 1]
+            middle_s[...] = mm(phi_s[NY - 1], xb_s[...]) + beta_s[NY - 1]
             for n in range(2):
                 middle_copy(n).start()
 
         @pl.when((group == 0) & (rank == 0))
         def _():
-            state = own_s[0, 1]
+            state = beta_s[NY - 1]
             for i in range(1, NG):
-                arrived(zab_s.at[i], zab_sem.at[i])
+                arrived(zab_s.at[i, 1], zab_sem.at[NG + i])
                 state = mm(zab_s[i, 0], state) + zab_s[i, 1]
             middle_s[...] = state
             for n in range(2):
                 middle_copy(n).start()
 
-        sout_s[0] = x_s[:, dim:]
-        later = mm(jnp.concatenate([phi_s[i] for i in range(NY - 1)], axis=0), x_s[...])
+        sout_s[0] = xb_s[...]
+        later = mm(phis, xb_s[...])
         for i in range(1, NY):
-            sout_s[i] = later[(i - 1) * dim:i * dim, dim:] + beta_s[i - 1]
+            sout_s[i] = later[(i - 1) * dim:i * dim] + beta_s[i - 1]
 
         @pl.when(group == 1)
         def _():
             arrived(mid_s, mid_sem)
-            stack = jnp.concatenate([x_s[:, :dim], later[:, :dim]], axis=0)
-            more = mm(stack, mid_s[...])
+            more = mm(xa_s[...], mid_s[...])
             for i in range(NY):
                 sout_s[i] = sout_s[i] + more[i * dim:(i + 1) * dim]
 
-        for i in range(NY):
+        for i in near_first[::-1]:
             remote(sout_s.at[i], sin_s.at[y], send_sem.at[28 + i], sin_sem.at[y], dev(z, i, 0)).start()
         for dlt in range(1, NZ):
             @pl.when(z >= dlt)
@@ -371,7 +398,7 @@
         psi_s[NY - 2] = aown_s[NY - 1]
         for i in range(NY - 3, -1, -1):
             psi_s[i] = mm(psi_s[i + 1], aown_s[i + 1])
-        for h in range(heads):
+        for h in near_first:
             arrived(sin_s.at[h], sin_sem.at[h])
             s1_s[h] = mm(ab_s[h, 0], sin_s[h]) + ab_s[h, 1]
             remote(s1_s.at[h], sin_s.at[h], send_sem.at[28 + h], sin_sem.at[h], pair).start()
@@ -394,8 +421,9 @@
     for h in range(heads):
         c_s[h] = mm(rt_s[h], adj_s[h])
 
-        @pl.when(c == 1)
-        def _():
+    @pl.when(c == 1)
+    def _():
+        for h in near_first[::-1]:
             remote(c_s.at[h], cpair_s.at[h], send_sem.at[32 + h], cpair_sem.at[h], pair).start()
 
     gpart_s[...] = jnp.broadcast_to(gain_part, (8, dim))
@@ -419,6 +447,14 @@
             gz_copy(d).start()
         gz_s[z] = gsum_s[0]
 
+    def gain_along_x():
+        for d in range(1, NZ):
+            arrived(gz_s.at[(z + NZ - d) % NZ], gz_sem.at[d - 1])
+        gsum_s[1] = jnp.sum(gz_s[...], axis=0)
+        for d in range(1, 4):
+            gx_copy(d).start()
+        gx_s[xpos] = gsum_s[1]
+
     def gz_copy(d):
         return remote(
             gsum_s.at[0], gz_s.at[z], gsend_sem.at[6 + d], gz_sem.at[d - 1], dev((z + d) % NZ, y, c)
@@ -431,16 +467,12 @@
 
     @pl.when(c == 0)
     def _():
-        for h in range(heads):
+        for h in near_first[::-1]:
             arrived(cpair_s.at[h], cpair_sem.at[h])
             cc_s[h] = mm(ab_s[h, 0], cpair_s[h], 0, 0) + c_s[h]
-
-            @pl.when(y == h)
-            def _():
+            if h is near_first[0]:
                 pltpu.make_async_copy(cc_s.at[h], cown_s.at[h], cown_sem.at[h]).start()
-
-            @pl.when(y != h)
-            def _():
+            else:
                 remote(cc_s.at[h], cown_s.at[y], send_sem.at[32 + h], cown_sem.at[y], dev(z, h, 0)).start()
         for i in range(NY):
             arrived(cown_s.at[i], cown_sem.at[i])
@@ -469,6 +501,7 @@
         def _():
             arrived(za_s.at[NZ - 2], za_sem.at[NZ - 2])
 
+        gain_along_x()
         for dlt in range(NZ - 1, 0, -1):
             @pl.when(z + dlt < NZ)
             def _():
@@ -479,7 +512,7 @@
         dsend_s[NY - 1] = d_row
         for i in range(NY - 1):
             dsend_s[i] = mm(psi_s[i], d_row, 0, 0) + gam_s[i]
-        for i in range(NY):
+        for i in near_first[::-1]:
             remote(dsend_s.at[i], dout_s.at[y], send_sem.at[12 + i], dout_sem.at[y], dev(z, i, 1)).start()
         for h in range(heads):
             arrived(dout_s.at[h], dout_sem.at[h])
@@ -488,17 +521,11 @@
     def _():
         gain_along_z()
         fill_backward()
-        for h in range(heads):
+        gain_along_x()
+        for h in near_first:
             arrived(dout_s.at[h], dout_sem.at[h])
             d0_s[h] = mm(ab_s[h, 0], dout_s[h], 0, 0) + c_s[h]
             remote(d0_s.at[h], dout_s.at[h], send_sem.at[36 + h], dout_sem.at[h], pair).start()
-
-    for d in range(1, NZ):
-        arrived(gz_s.at[(z + NZ - d) % NZ], gz_sem.at[d - 1])
-    gsum_s[1] = jnp.sum(gz_s[...], axis=0)
-    for d in range(1, 4):
-        gx_copy(d).start()
-    gx_s[xpos] = gsum_s[1]
 
     lane = lax.broadcasted_iota(jnp.int32, (steps, heads), 1)
     db_all = jnp.zeros((steps, heads), F32)
@@ -529,25 +556,19 @@
 
     for j in range(2):
         send["pair", j].wait_send()
-        head = 2 * c + j
-
-        @pl.when(jnp.logical_not((c == 1) & (y == head)))
-        def _():
-            remote(comp_s.at[j], own_s.at[y], send_sem.at[2 + j], own_sem.at[y], dev(z, head, 1)).wait_send()
+
+        @pl.when(jnp.logical_not(own_here(j)))
+        def _():
+            own_copy(j, 0).wait_send()
+            own_copy(j, 1).wait_send()
 
     def left(src, sem):
         remote(src, src, sem, sem, pair).wait_send()
 
     @pl.when(c == 1)
     def _():
-        for dlt in range(1, NG):
-            @pl.when(rank + dlt < NG)
-            def _():
-                zab_copy(dlt).wait_send()
-
-        @pl.when((group == 0) & (rank > 0))
-        def _():
-            zback_copy().wait_send()
+        for part in range(2):
+            zab_each(part, lambda copy: copy.wait_send())
 
         @pl.when((z == 0) | (z == NG - 1))
         def _():
@@ -568,12 +589,10 @@
 
     @pl.when(c == 0)
     def _():
-        for h in range(heads):
+        for h in near_first:
             left(s1_s.at[h], send_sem.at[28 + h])
-
-            @pl.when(y != h)
-            def _():
-                left(cc_s.at[h], send_sem.at[32 + h])
+        for h in near_first[1:]:
+            left(cc_s.at[h], send_sem.at[32 + h])
         for dlt in range(1, NZ):
             @pl.when(z >= dlt)
             def _():
@@ -612,8 +631,8 @@
         f(heads, dim, dim), f(heads, dim, dim), f(NY, dim, dim), f(dim, dim), f(NZ - 1, dim, dim),
         f(NY - 1, dim, dim), f(NY, dim, dim), f(heads, dim, dim), f(heads, dim, dim),
         f(8, dim), f(NY * NC, 8, dim), f(NZ, 8, dim), f(4, 8, dim), f(2, 8, dim),
-        f(dim, 2 * dim), f(dim, dim), f(dim, dim), dma,
-        dma((40,)), dma((2,)), dma((NY,)), dma((NG,)), dma((NZ - 1,)), dma((heads,)), dma((2 * NY,)),
+        f(NY * dim, dim), f(dim, dim), f(dim, dim), f(dim, dim), dma,
+        dma((48,)), dma((2,)), dma((2 * NY,)), dma((2 * NG,)), dma((NZ - 1,)), dma((heads,)), dma((2 * NY,)),
         dma((heads,)), dma((NY,)), dma((NZ - 1,)), dma((heads,)),
         dma((24,)), dma((NY * NC - 1,)), dma((NZ - 1,)), dma((3,)),
     ]

time: 59.9 us -> 58.4 us (0.975); the launches traced: 59 us -> 58.3 us
  Pallas kernels: 58.2 us -> 57.5 us
    pallas_call x1, Pallas kernels: 57.3 us -> 56.5 us  [local(): pl.pallas_call(kernel, out_shape=(jax.ShapeDtypeStruct((tok * heads, dim)...]
where the time goes in v5:
time: 58.4 us; the launch traced here: 58.3 us
  Pallas kernels  57.5 us (98%)
  between operations  0.8 us (1%)
    pallas_call x1, Pallas kernels, local(): pl.pallas_call(kernel, out_shape=(jax.ShapeDtypeStruct((tok * heads, dim)...  56.5 us

profile of v5, /device:TPU:32, one launch (start us, length us, event | category | flops | bytes accessed | tf_op | source)
XLA Modules:
  0.0 58.3 jit_solution(5638708290958348783)
XLA Ops:
  0.6 56.5 %delta_product.1 = (bf16[512,128]{1,0:T(8,128)(2,1)S(1)}, bf16[512,128]{1,0:T(8,128)(2,1)S(1)}, bf16[1024,128]{1,0:T(8,128)(2,1)S(1)}, bf16[1024,128]{1,0:T(8,12...) custom-call(bf16[512,128]{1,0:T(8,128)(2,1)} %bitcast.18, bf16[1024,128]{1,0:T(8,128)(2,1)} %bitcast.16, ...), custom_call_target="tpu_custom_call" | custom-call | tf_op jit(solution)/shard_map/delta_product/pallas_call | solution.py:639
  57.2 0.9 %store.1 = (bf16[512,128]{1,0:T(8,128)(2,1)}, bf16[512,128]{1,0:T(8,128)(2,1)}, bf16[1024,128]{1,0:T(8,128)(2,1)}, bf16[1024,128]{1,0:T(8,128)(2,1)}, f32[8,128]{1,0:T(8,128)}, /*index=5*/f32[1,128]{1,0:T(1,128)}) custom-call(bf16[512,128]{1,0:T(8,128)(2,1)S(1)} %get-tuple-element.18.refs_0_, bf16[512,128]{1,0:T(8,128)(2,1)S(1)} %get-tuple-element.19.refs_1_, ...), custom_call_target="tpu_custom_call" | custom-call | tf_op jit(solution)/shard_map/store/pallas_call | solution.py:667

commit v6 on v5

--- a/solution.py
+++ b/solution.py
@@ -56,7 +56,7 @@
     g0_s, dk1_s, of_s, dq_s, dk_s, dvf_s, dv_s,
     ab_s, pair_s, comp_s, own_s, phi_s, beta_s, zab_s, za_s, sout_s, sin_s, s1_s,
     aown_s, phi0_s, theta_s, psi_s, c_s, cpair_s, cc_s, cown_s, crow_s, zc_s, gam_s, dsend_s, dout_s, d0_s,
-    gpart_s, grow_s, gz_s, gx_s, gsum_s, xa_s, xb_s, middle_s, mid_s, mid_sem,
+    gpart_s, grow_s, gz_s, gx_s, gsum_s, xa_s, xb_s, middle_s, mid_s, mid_sem, at_s, psit_s, phit_s, thetat_s,
     send_sem, pair_sem, own_sem, zab_sem, za_sem, sin_sem, aown_sem, cpair_sem, cown_sem, zc_sem, dout_sem,
     gsend_sem, grow_sem, gz_sem, gx_sem,
 ):
@@ -176,16 +176,11 @@
     turned = bt_ref[...].T
     for j in range(per):
         b_ref[pl.ds(j, tok, stride=per), :] = turned[:, j * heads:(j + 1) * heads]
-    q = q_ref[...].astype(F32)
     k = k_ref[...].astype(F32)
-    rq = lax.rsqrt(jnp.sum(q * q, axis=-1, keepdims=True) + EPS)
     rk = lax.rsqrt(jnp.sum(k * k, axis=-1, keepdims=True) + EPS)
-    rq_s[...] = rq
     rk_s[...] = rk
-    qu_s[...] = q * rq
     ku_s[...] = k * rk
     vf_s[...] = v_ref[...].astype(F32)
-    dof_s[...] = do_ref[...].astype(F32)
 
     def of_head(ref, h, rows):
         return ref[pl.ds(h, rows, stride=heads), :]
@@ -251,7 +246,13 @@
         ab_s[h, 1] = ab[:, dim:]
 
     def fill_forward():
+        q = q_ref[...].astype(F32)
+        rq = lax.rsqrt(jnp.sum(q * q, axis=-1, keepdims=True) + EPS)
+        rq_s[...] = rq
+        qu_s[...] = q * rq
+        dof_s[...] = do_ref[...].astype(F32)
         for h in range(heads):
+            at_s[h] = ab_s[h, 0].T
             ku = of_head(ku_s, h, steps)
             qu = of_head(qu_s, h, tok)
             sc = jnp.where(visible, mm(qu, ku, 1, 1), 0.0)
@@ -398,6 +399,9 @@
         psi_s[NY - 2] = aown_s[NY - 1]
         for i in range(NY - 3, -1, -1):
             psi_s[i] = mm(psi_s[i + 1], aown_s[i + 1])
+        for i in range(NY - 1):
+            psit_s[i * dim:(i + 1) * dim] = psi_s[i].T
+            phit_s[:, i * dim:(i + 1) * dim] = phi0_s[i + 1].T
         for h in near_first:
             arrived(sin_s.at[h], sin_sem.at[h])
             s1_s[h] = mm(ab_s[h, 0], sin_s[h]) + ab_s[h, 1]
@@ -469,16 +473,15 @@
     def _():
         for h in near_first[::-1]:
             arrived(cpair_s.at[h], cpair_sem.at[h])
-            cc_s[h] = mm(ab_s[h, 0], cpair_s[h], 0, 0) + c_s[h]
+            cc_s[h] = mm(at_s[h], cpair_s[h]) + c_s[h]
             if h is near_first[0]:
                 pltpu.make_async_copy(cc_s.at[h], cown_s.at[h], cown_sem.at[h]).start()
             else:
                 remote(cc_s.at[h], cown_s.at[y], send_sem.at[32 + h], cown_sem.at[y], dev(z, h, 0)).start()
         for i in range(NY):
             arrived(cown_s.at[i], cown_sem.at[i])
-        left = jnp.concatenate([phi0_s[i] for i in range(1, NY)], axis=0)
         right = jnp.concatenate([cown_s[i] for i in range(1, NY)], axis=0)
-        crow_s[...] = cown_s[0] + mm(left, right, 0, 0)
+        crow_s[...] = cown_s[0] + mm(phit_s[...], right)
         for dlt in range(NZ - 1, 0, -1):
             @pl.when(z >= dlt)
             def _():
@@ -496,6 +499,7 @@
                 arrived(za_s.at[dlt - 1], za_sem.at[dlt - 1])
 
             theta_s[dlt] = za_s[0] if dlt == 1 else mm(za_s[dlt - 1], theta_s[dlt - 1])
+            thetat_s[:, (dlt - 1) * dim:dlt * dim] = theta_s[dlt].T
 
         @pl.when(z + NZ - 1 < NZ)
         def _():
@@ -506,12 +510,12 @@
             @pl.when(z + dlt < NZ)
             def _():
                 arrived(zc_s.at[dlt - 1], zc_sem.at[dlt - 1])
-        left = jnp.concatenate([theta_s[i] for i in range(1, NZ - 1)], axis=0)
         right = jnp.concatenate([zc_s[i] for i in range(1, NZ - 1)], axis=0)
-        d_row = zc_s[0] + mm(left, right, 0, 0)
+        d_row = zc_s[0] + mm(thetat_s[...], right)
         dsend_s[NY - 1] = d_row
+        more = mm(psit_s[...], d_row)
         for i in range(NY - 1):
-            dsend_s[i] = mm(psi_s[i], d_row, 0, 0) + gam_s[i]
+            dsend_s[i] = more[i * dim:(i + 1) * dim] + gam_s[i]
         for i in near_first[::-1]:
             remote(dsend_s.at[i], dout_s.at[y], send_sem.at[12 + i], dout_sem.at[y], dev(z, i, 1)).start()
         for h in range(heads):
@@ -524,7 +528,7 @@
         gain_along_x()
         for h in near_first:
             arrived(dout_s.at[h], dout_sem.at[h])
-            d0_s[h] = mm(ab_s[h, 0], dout_s[h], 0, 0) + c_s[h]
+            d0_s[h] = mm(at_s[h], dout_s[h]) + c_s[h]
             remote(d0_s.at[h], dout_s.at[h], send_sem.at[36 + h], dout_sem.at[h], pair).start()
 
     lane = lax.broadcasted_iota(jnp.int32, (steps, heads), 1)
@@ -632,6 +636,7 @@
         f(NY - 1, dim, dim), f(NY, dim, dim), f(heads, dim, dim), f(heads, dim, dim),
         f(8, dim), f(NY * NC, 8, dim), f(NZ, 8, dim), f(4, 8, dim), f(2, 8, dim),
         f(NY * dim, dim), f(dim, dim), f(dim, dim), f(dim, dim), dma,
+        f(heads, dim, dim), f((NY - 1) * dim, dim), f(dim, (NY - 1) * dim), f(dim, (NZ - 2) * dim),
         dma((48,)), dma((2,)), dma((2 * NY,)), dma((2 * NG,)), dma((NZ - 1,)), dma((heads,)), dma((2 * NY,)),
         dma((heads,)), dma((NY,)), dma((NZ - 1,)), dma((heads,)),
         dma((24,)), dma((NY * NC - 1,)), dma((NZ - 1,)), dma((3,)),

time: 58.4 us -> 57.9 us (level)
  no operation moved by 1% of the time
where the time goes in v6:
time: 57.9 us; the launch traced here: 57.8 us
  Pallas kernels  57 us (98%)
  between operations  0.8 us (1%)
    pallas_call x1, Pallas kernels, local(): pl.pallas_call(kernel, out_shape=(jax.ShapeDtypeStruct((tok * heads, dim)...  56.1 us

profile of v6, /device:TPU:32, one launch (start us, length us, event | category | flops | bytes accessed | tf_op | source)
XLA Modules:
  0.0 57.8 jit_solution(17300348252255595443)
XLA Ops:
  0.6 56.1 %delta_product.1 = (bf16[512,128]{1,0:T(8,128)(2,1)S(1)}, bf16[512,128]{1,0:T(8,128)(2,1)S(1)}, bf16[1024,128]{1,0:T(8,128)(2,1)S(1)}, bf16[1024,128]{1,0:T(8,12...) custom-call(bf16[512,128]{1,0:T(8,128)(2,1)} %bitcast.18, bf16[1024,128]{1,0:T(8,128)(2,1)} %bitcast.16, ...), custom_call_target="tpu_custom_call" | custom-call | tf_op jit(solution)/shard_map/delta_product/pallas_call | solution.py:644
  56.7 0.9 %store.1 = (bf16[512,128]{1,0:T(8,128)(2,1)}, bf16[512,128]{1,0:T(8,128)(2,1)}, bf16[1024,128]{1,0:T(8,128)(2,1)}, bf16[1024,128]{1,0:T(8,128)(2,1)}, f32[8,128]{1,0:T(8,128)}, /*index=5*/f32[1,128]{1,0:T(1,128)}) custom-call(bf16[512,128]{1,0:T(8,128)(2,1)S(1)} %get-tuple-element.18.refs_0_, bf16[512,128]{1,0:T(8,128)(2,1)S(1)} %get-tuple-element.19.refs_1_, ...), custom_call_target="tpu_custom_call" | custom-call | tf_op jit(solution)/shard_map/store/pallas_call | solution.py:672

commit v7 on v6

--- a/solution.py
+++ b/solution.py
@@ -56,7 +56,7 @@
     g0_s, dk1_s, of_s, dq_s, dk_s, dvf_s, dv_s,
     ab_s, pair_s, comp_s, own_s, phi_s, beta_s, zab_s, za_s, sout_s, sin_s, s1_s,
     aown_s, phi0_s, theta_s, psi_s, c_s, cpair_s, cc_s, cown_s, crow_s, zc_s, gam_s, dsend_s, dout_s, d0_s,
-    gpart_s, grow_s, gz_s, gx_s, gsum_s, xa_s, xb_s, middle_s, mid_s, mid_sem, at_s, psit_s, phit_s, thetat_s,
+    gpart_s, grow_s, gz_s, gx_s, gsum_s, xa_s, xb_s, middle_s, mid_s, mid_sem, at_s, psit_s, phit_s, thetat_s, normal_s,
     send_sem, pair_sem, own_sem, zab_sem, za_sem, sin_sem, aown_sem, cpair_sem, cown_sem, zc_sem, dout_sem,
     gsend_sem, grow_sem, gz_sem, gx_sem,
 ):
@@ -239,7 +239,9 @@
     for h in range(heads):
         ku = of_head(ku_s, h, steps)
         b = b_ref[:, h:h + 1]
-        wu_s[h] = mm(n_s[h], jnp.concatenate([b * ku, b * of_head(vf_s, h, steps)], axis=1))
+        right = split(jnp.concatenate([b * ku, b * of_head(vf_s, h, steps)], axis=1))
+        wu_s[h, :half] = mms(split(n_s[h, :half, :half]), (right[0][:half], right[1][:half]))
+        wu_s[h, half:] = mms(split(n_s[h, half:]), right)
     for h in range(heads):
         ab = mm(of_head(ku_s, h, steps).T, wu_s[h])
         ab_s[h, 0] = eye_dim - ab[:, :dim]
@@ -268,6 +270,9 @@
 
     def fill_backward():
         for h in range(heads):
+            of_s[pl.ds(h, tok, stride=heads), :] = g_ref[...] * normal_s[h]
+            p_s[h] = wu_s[h, :, dim:] - mm(wu_s[h, :, :dim], sin_s[h])
+        for h in range(heads):
             ku = of_head(ku_s, h, steps)
             adj = adj_s[h]
             m_do = jnp.where(visible, mm(adj, p_s[h], 1, 1), 0.0)
@@ -410,16 +415,13 @@
     gain = g_ref[...]
     gain_part = jnp.zeros((1, dim), F32)
     for h in range(heads):
-        both = mm(jnp.concatenate([r_s[h], wu_s[h, :, :dim]], axis=0), sin_s[h])
-        ol_s[h] = ol_s[h] + both[:tok]
-        p_s[h] = wu_s[h, :, dim:] - both[tok:]
+        ol_s[h] = ol_s[h] + mm(r_s[h], sin_s[h])
     for h in range(heads):
         o = ol_s[h]
         inv_rms = lax.rsqrt(jnp.mean(o * o, axis=-1, keepdims=True) + EPS)
         normal = o * inv_rms
         grad = of_head(dof_s, h, tok)
-        of_s[pl.ds(h, tok, stride=heads), :] = gain * normal
-        gain_part = gain_part + jnp.sum(grad * normal, axis=0, keepdims=True)
+        normal_s[h] = normal
         scaled = grad * gain
         adj_s[h] = inv_rms * (scaled - normal * jnp.mean(scaled * normal, axis=-1, keepdims=True))
     for h in range(heads):
@@ -430,6 +432,8 @@
         for h in near_first[::-1]:
             remote(c_s.at[h], cpair_s.at[h], send_sem.at[32 + h], cpair_sem.at[h], pair).start()
 
+    for h in range(heads):
+        gain_part = gain_part + jnp.sum(of_head(dof_s, h, tok) * normal_s[h], axis=0, keepdims=True)
     gpart_s[...] = jnp.broadcast_to(gain_part, (8, dim))
     me8 = y * NC + c
     n_g = 0
@@ -542,6 +546,7 @@
         db = jnp.sum(gm * p_s[h], axis=-1, keepdims=True) / b
         db_all = db_all + jnp.where(lane == h, db, 0.0)
     db_s[...] = db_all
+    dv_ref[...] = dvf_s[...].astype(BF16)
     for h in range(heads):
         hm = jnp.where(col_i < row_i, mm(dv_s[h], p_s[h], 1, 1), 0.0)
         low_s[h] = hm + hm.T
@@ -552,7 +557,6 @@
         dk_s[pl.ds(h, steps, stride=heads), :] = dk
     db_ref[...] = jnp.concatenate([db_s[pl.ds(j, tok, stride=per), :] for j in range(per)], axis=1).T
     dk_ref[...] = unit_pullback(dk_s[...], ku_s[...], rk_s[...]).astype(BF16)
-    dv_ref[...] = dvf_s[...].astype(BF16)
 
     for d in range(1, 4):
         arrived(gx_s.at[(xpos + 4 - d) % 4], gx_sem.at[d - 1])
@@ -636,7 +640,7 @@
         f(NY - 1, dim, dim), f(NY, dim, dim), f(heads, dim, dim), f(heads, dim, dim),
         f(8, dim), f(NY * NC, 8, dim), f(NZ, 8, dim), f(4, 8, dim), f(2, 8, dim),
         f(NY * dim, dim), f(dim, dim), f(dim, dim), f(dim, dim), dma,
-        f(heads, dim, dim), f((NY - 1) * dim, dim), f(dim, (NY - 1) * dim), f(dim, (NZ - 2) * dim),
+        f(heads, dim, dim), f((NY - 1) * dim, dim), f(dim, (NY - 1) * dim), f(dim, (NZ - 2) * dim), f(heads, tok, dim),
         dma((48,)), dma((2,)), dma((2 * NY,)), dma((2 * NG,)), dma((NZ - 1,)), dma((heads,)), dma((2 * NY,)),
         dma((heads,)), dma((NY,)), dma((NZ - 1,)), dma((heads,)),
         dma((24,)), dma((NY * NC - 1,)), dma((NZ - 1,)), dma((3,)),

time: 57.9 us -> 57.8 us (level)
  no operation moved by 1% of the time
where the time goes in v7:
time: 57.8 us; the launch traced here: 57.7 us
  Pallas kernels  56.9 us (98%)
  between operations  0.8 us (1%)
    pallas_call x1, Pallas kernels, local(): pl.pallas_call(kernel, out_shape=(jax.ShapeDtypeStruct((tok * heads, dim)...  55.9 us

profile of v7, /device:TPU:32, one launch (start us, length us, event | category | flops | bytes accessed | tf_op | source)
XLA Modules:
  0.0 57.7 jit_solution(17758138509543842955)
XLA Ops:
  0.6 55.9 %delta_product.1 = (bf16[512,128]{1,0:T(8,128)(2,1)S(1)}, bf16[512,128]{1,0:T(8,128)(2,1)S(1)}, bf16[1024,128]{1,0:T(8,128)(2,1)S(1)}, bf16[1024,128]{1,0:T(8,12...) custom-call(bf16[512,128]{1,0:T(8,128)(2,1)} %bitcast.18, bf16[1024,128]{1,0:T(8,128)(2,1)} %bitcast.16, ...), custom_call_target="tpu_custom_call" | custom-call | tf_op jit(solution)/shard_map/delta_product/pallas_call | solution.py:648
  56.6 0.9 %store.1 = (bf16[512,128]{1,0:T(8,128)(2,1)}, bf16[512,128]{1,0:T(8,128)(2,1)}, bf16[1024,128]{1,0:T(8,128)(2,1)}, bf16[1024,128]{1,0:T(8,128)(2,1)}, f32[8,128]{1,0:T(8,128)}, /*index=5*/f32[1,128]{1,0:T(1,128)}) custom-call(bf16[512,128]{1,0:T(8,128)(2,1)S(1)} %get-tuple-element.18.refs_0_, bf16[512,128]{1,0:T(8,128)(2,1)S(1)} %get-tuple-element.19.refs_1_, ...), custom_call_target="tpu_custom_call" | custom-call | tf_op jit(solution)/shard_map/store/pallas_call | solution.py:676
